TPU v7x, 128 devices: a whole 4x4x4 slice. The times are simulated.
128 devices in a mesh: rows: 128 (over z, x, y, core).
Axes of the slice: x: 4, y: 4, z: 4, core: 2. Of those that a mesh axis runs over, the one named last changes fastest.
Arguments:
- features: bfloat16 [131072, 1024], P('rows'), may hold values from -6 to 6
- flip_signs: int32 [131072], P('rows'), may hold values from -1 to 1, as said below
- sample_rows: int32 [4096], P('rows'), may hold values from 0 to 131071, as said below
Outputs:
- sketch: float32 [4096, 1024], P('rows')
- upper_factor: float32 [1024, 1024], replicated
- leverage: float32 [131072], P('rows')
Inputs may be any that keep to these rules, and one draw needn't show every extreme that they name: `flip_signs`: every entry is -1 or 1. `sample_rows`: strictly increasing, with exactly 32 indices in each aligned block of 1024 rows; cut each such block into consecutive groups of 8 rows: every group holds at most max(1, 32 / 128) indices, and 32 / max(1, 32 / 128) groups of each block hold exactly that many.
All inputs are finite; a program needn't handle non-finite values.
Results may differ from a plain program's by a relative error of at most 0.004.
Values may be sent and summed in bfloat16 or wider, within the bound.
No kernel may reach another device: no remote copies, remote signals or barrier semaphores. Data moves between devices by JAX's collectives and lax.ppermute only.
A program may use at most 128 MiB of HBM per device.

v0:
```python
import math

import jax
import jax.numpy as jnp
from jax import lax
from jax.sharding import PartitionSpec as P

FACTOR = 128
SAMPLES = 4096


def hadamard_table(dimension):
    positions = jnp.arange(dimension, dtype=jnp.int32)
    common_bits = positions[:, None] & positions[None, :]
    parity = jnp.zeros((dimension, dimension), jnp.int32)
    for bit_pos in range(max(dimension.bit_length() - 1, 0)):
        parity = parity + (common_bits >> bit_pos & 1)
    return (1 - 2 * (parity % 2)).astype(jnp.float32)


def local_transform(features, flip_signs):
    rows_dev, columns = features.shape
    flipped = features * flip_signs.astype(jnp.bfloat16)[:, None]
    inner_table = hadamard_table(FACTOR).astype(jnp.bfloat16)
    outer_table = hadamard_table(rows_dev // FACTOR).astype(jnp.bfloat16)
    grouped = flipped.reshape(rows_dev // FACTOR, FACTOR, columns)
    section_one = jnp.einsum(
        "ka,bac->bkc", inner_table, grouped, preferred_element_type=jnp.float32
    ).astype(jnp.bfloat16)
    section_two = jnp.einsum(
        "jb,bkc->jkc", outer_table, section_one, preferred_element_type=jnp.float32
    ).astype(jnp.bfloat16)
    return section_two.reshape(rows_dev, columns)


def shards(features, flip_signs, sample_rows):
    rows_dev, columns = features.shape
    group_size = lax.axis_size("rows")
    position = lax.axis_index("rows")
    shrink = 1.0 / math.sqrt(SAMPLES)
    mixed_rows = local_transform(features, flip_signs)
    table = hadamard_table(group_size).astype(jnp.bfloat16)
    pieces = mixed_rows.reshape(group_size, rows_dev // group_size, columns)
    summed = (
        jnp.einsum(
            "ed,dqc->eqc",
            table,
            lax.all_to_all(pieces, "rows", split_axis=0, concat_axis=0, tiled=True),
            preferred_element_type=jnp.float32,
        )
        * shrink
    )
    sketched = lax.all_to_all(summed, "rows", split_axis=0, concat_axis=0, tiled=True)
    sketched = sketched.reshape(rows_dev, columns)
    local_rows = sample_rows - position * rows_dev
    sketch = jnp.take(sketched, local_rows, axis=0)
    all_rows = lax.all_gather(sketch, "rows", axis=0, tiled=True)
    gram_matrix = jnp.dot(all_rows.T, all_rows, precision=lax.Precision.HIGHEST)
    lower_factor = jnp.linalg.cholesky(gram_matrix)
    upper_factor = lower_factor.T
    solved = jax.scipy.linalg.solve_triangular(
        lower_factor, features.astype(jnp.float32).T, lower=True
    )
    leverage = jnp.sum(solved * solved, axis=0) * (rows_dev * group_size / columns)
    return (sketch, upper_factor, leverage)


def solution(mesh):
    placed = (P("rows", None), P("rows"), P("rows"))
    return jax.shard_map(
        shards,
        mesh=mesh,
        in_specs=placed,
        out_specs=(P("rows", None), P(), P("rows")),
        check_vma=False,
    )
```

profile of v0, /device:TPU:1, one launch (start us, length us, event | category | flops | bytes accessed | tf_op | source)
XLA Modules:
  0.0 624.5 jit_solution(6688591097272219167)
XLA Ops:
  10.5 2.9 copy.14
  16.8 41.4 %all_to_all.10 = bf16[128,8,1024]{2,1,0:T(8,128)(2,1)S(1)} all-to-all(bf16[128,8,1024]{2,1,0:T(8,128)(2,1)S(1)} %bitcast.123), channel_id=1, replica_groups=mesh['rows'=128] {'rows'}, dimensions={0} | all-to-all | bytes 4194304 | tf_op jit(solution)/shard_map/all_to_all | solution.py:48
  61.0 4.4 copy.17
  65.5 6.0 all-to-all-start.1
  71.6 52.8 %all-to-all-done.1 = f32[128,8,1024]{2,1,0:T(8,128)} async-done(((f32[128,8,1024]{2,1,0:T(8,128)}), f32[128,8,1024]{2,1,0:T(8,128)}, u32[]{:S(2)}, u32[]{:S(2)}) %all-to-all-start.1) | async-done | bytes 4194336 | tf_op jit(solution)/shard_map/all_to_all | solution.py:53
  124.3 2.9 gather_fusion
  128.0 2.9 copy.19
  133.2 70.8 %all-gather.2.cloned.1.call-done = f32[4096,1024]{1,0:T(8,128)} async-done(((f32[32,1024]{1,0:T(8,128)}), f32[4096,1024]{1,0:T(8,128)}) %all-gather.2.cloned.1.call-update) | async-done | bytes 16777232 | tf_op jit(solution)/shard_map/all_gather | solution.py:57
  204.0 62.0 %fusion.114 = f32[1024,1024]{1,0:T(8,128)} fusion(f32[4096,1024]{1,0:T(8,128)} %all-gather.2.cloned.1.call-done), kind=kOutput, calls=%fused_computation.216 | convolution fusion | flops 51539607552 | bytes 20971520 | tf_op jit(solution)/shard_map/dot_general | solution.py:58
  266.1 5.4 copy.18
  271.4 4.4 fusion
  277.8 11.7 %cholesky.223 = f32[128,128]{1,0:T(8,128)S(1)} custom-call(f32[128,128]{1,0:T(8,128)S(1)} %cholesky.580), custom_call_target="Cholesky" | custom-call | tf_op jit(solution)/shard_map/jit(cholesky)/cholesky | solution.py:59
  289.6 9.8 %custom-call.63 = f32[1,128,128]{1,2,0:T(8,128)S(1)} custom-call(f32[1,128,128]{2,1,0:T(8,128)S(1)} %get-tuple-element.80), custom_call_target="InvertDiagBlocksLowerTriangular" | custom-call | tf_op jit(solution)/shard_map/jit(cholesky)/cholesky | solution.py:59
  305.8 11.9 %cholesky.244 = f32[128,128]{1,0:T(8,128)S(1)} custom-call(f32[128,128]{1,0:T(8,128)S(1)} %cholesky.584), custom_call_target="Cholesky" | custom-call | tf_op jit(solution)/shard_map/jit(cholesky)/cholesky | solution.py:59
  318.3 9.8 %custom-call.64 = f32[1,128,128]{1,2,0:T(8,128)S(1)} custom-call(f32[1,128,128]{2,1,0:T(8,128)S(1)} %get-tuple-element.77), custom_call_target="InvertDiagBlocksLowerTriangular" | custom-call | tf_op jit(solution)/shard_map/jit(cholesky)/cholesky | solution.py:59
  331.4 11.7 %cholesky.468 = f32[128,128]{1,0:T(8,128)S(1)} custom-call(f32[128,128]{1,0:T(8,128)S(1)} %cholesky.589), custom_call_target="Cholesky" | custom-call | tf_op jit(solution)/shard_map/jit(cholesky)/cholesky | solution.py:59
  344.4 9.8 %custom-call.65 = f32[1,128,128]{1,2,0:T(8,128)S(1)} custom-call(f32[1,128,128]{2,1,0:T(8,128)S(1)} %get-tuple-element.74), custom_call_target="InvertDiagBlocksLowerTriangular" | custom-call | tf_op jit(solution)/shard_map/jit(cholesky)/cholesky | solution.py:59
  357.7 11.9 %cholesky.487 = f32[128,128]{1,0:T(8,128)S(1)} custom-call(f32[128,128]{1,0:T(8,128)S(1)} %cholesky.594), custom_call_target="Cholesky" | custom-call | tf_op jit(solution)/shard_map/jit(cholesky)/cholesky | solution.py:59
  370.9 9.8 %custom-call.66 = f32[1,128,128]{1,2,0:T(8,128)S(1)} custom-call(f32[1,128,128]{2,1,0:T(8,128)S(1)} %get-tuple-element.71), custom_call_target="InvertDiagBlocksLowerTriangular" | custom-call | tf_op jit(solution)/shard_map/jit(cholesky)/cholesky | solution.py:59
  384.2 11.7 %cholesky.506 = f32[128,128]{1,0:T(8,128)S(1)} custom-call(f32[128,128]{1,0:T(8,128)S(1)} %cholesky.599), custom_call_target="Cholesky" | custom-call | tf_op jit(solution)/shard_map/jit(cholesky)/cholesky | solution.py:59
  397.2 10.2 %custom-call.67 = f32[1,128,128]{1,2,0:T(8,128)S(1)} custom-call(f32[1,128,128]{2,1,0:T(8,128)S(1)} %get-tuple-element.68), custom_call_target="InvertDiagBlocksLowerTriangular" | custom-call | tf_op jit(solution)/shard_map/jit(cholesky)/cholesky | solution.py:59
  410.7 11.7 %cholesky.526 = f32[128,128]{1,0:T(8,128)S(1)} custom-call(f32[128,128]{1,0:T(8,128)S(1)} %cholesky.604), custom_call_target="Cholesky" | custom-call | tf_op jit(solution)/shard_map/jit(cholesky)/cholesky | solution.py:59
  423.7 9.8 %custom-call.68 = f32[1,128,128]{1,2,0:T(8,128)S(1)} custom-call(f32[1,128,128]{2,1,0:T(8,128)S(1)} %get-tuple-element.65), custom_call_target="InvertDiagBlocksLowerTriangular" | custom-call | tf_op jit(solution)/shard_map/jit(cholesky)/cholesky | solution.py:59
  436.5 11.9 %cholesky.546 = f32[128,128]{1,0:T(8,128)S(1)} custom-call(f32[128,128]{1,0:T(8,128)S(1)} %cholesky.609), custom_call_target="Cholesky" | custom-call | tf_op jit(solution)/shard_map/jit(cholesky)/cholesky | solution.py:59
  449.6 9.8 %custom-call.69 = f32[1,128,128]{1,2,0:T(8,128)S(1)} custom-call(f32[1,128,128]{2,1,0:T(8,128)S(1)} %get-tuple-element.62), custom_call_target="InvertDiagBlocksLowerTriangular" | custom-call | tf_op jit(solution)/shard_map/jit(cholesky)/cholesky | solution.py:59
  462.1 11.7 %cholesky.564 = f32[128,128]{1,0:T(8,128)S(1)} custom-call(f32[128,128]{1,0:T(8,128)S(1)} %convolution_subtract_fusion.11), custom_call_target="Cholesky" | custom-call | tf_op jit(solution)/shard_map/jit(cholesky)/cholesky | solution.py:59
  480.7 6.6 %fusion.1 = (f32[1024,1024]{1,0:T(8,128)}, f32[1024,1024]{0,1:T(8,128)}) fusion(f32[1024,1024]{1,0:T(8,128)} %get-tuple-element.60, pred[]{:T(512)S(6)} %cholesky.579), kind=kLoop, calls=%fused_computation.8 | loop fusion | flops 4194304 | bytes 12582913 | tf_op jit(solution)/shard_map/jit(_solve_triangular)/triangular_solve | solution.py:61
  487.3 5.3 copy.20
  492.6 23.0 %while.1 = (s32[]{:T(128)}, f32[1024,1024]{1,0:T(8,128)}, s32[8,2]{0,1:T(2,128)S(1)}, f32[8,128,128]{2,1,0:T(8,128)S(1)}, s32[]{:T(128)}) while((s32[]{:T(128)}, f32[1024,1024]{1,0:T(8,128)}, s32[8,2]{0,1:T(2,128)S(1)}, f32[8,128,128]{2,1,0:T(8,128)S(1)}, s32[]{:T(128)}) %tuple.66), condition=%wide.while_cond, body=%wide.while_body.sunk | while | flops 2 | bytes 131189 | solution.py:61
  515.6 78.8 %custom-call.70 = f32[8,128,128]{1,2,0:T(8,128)S(1)} custom-call(f32[8,128,128]{2,1,0:T(8,128)S(1)} %get-tuple-element.10), custom_call_target="InvertDiagBlocksLowerTriangular" | custom-call | tf_op jit(solution)/shard_map/jit(_solve_triangular)/triangular_solve | solution.py:61
  609.1 2.8 convolution_subtract_fusion.1
  612.6 3.3 convolution_subtract_fusion.3
  (97 shorter events, 88.9 us)
Async XLA Ops:
  65.5 6.0 copy-start.2
  65.5 58.8 %all-to-all-start.1 = ((f32[128,8,1024]{2,1,0:T(8,128)}), f32[128,8,1024]{2,1,0:T(8,128)}, u32[]{:S(2)}, u32[]{:S(2)}) async-start(f32[128,8,1024]{2,1,0:T(8,128)} %copy.17), calls=%async_computation.1 | async-start | bytes 8388608 | tf_op jit(solution)/shard_map/all_to_all | solution.py:53
  71.5 132.6 %all-gather.2.cloned.1.call-start = ((), (), s32[]{:S(2)}) async-start(), calls=%async_computation.2 | async-start | bytes 16908288 | tf_op jit(solution)/shard_map/all_gather | solution.py:57
  275.9 1.9 copy-start.1
  594.4 3.2 copy-start
Sparse Core Ops, SparseCore 0:
  128.1 75.9 all-gather.1
where the time goes:
time: 634 us; the launch traced here: 625 us
  other arithmetic  269 us (42%)
  waiting for transfers between devices  124 us (20%)
  matrix products  113 us (18%)
  local copies, waits for them, and re-layouts  52.3 us (8%)
  blocking collectives  41.4 us (7%)
  between operations  19.6 us (3%)
    another operation x30, other arithmetic, shards(): lower_factor = jnp.linalg.cholesky(gram_matrix)  172 us
    another operation x3, other arithmetic, shards(): jax.scipy.linalg.solve_triangular(lower_factor, features.astype(jnp.float...  85.4 us
    all_gather x1, waiting for transfers between devices, shards(): all_rows = lax.all_gather(sketch, 'rows', axis=0, tiled=True)  70.8 us
    dot_general x1, matrix products, shards(): gram_matrix = jnp.dot(all_rows.T, all_rows, precision=lax.Precision.HIGHEST)  62 us
    all_to_all x1, waiting for transfers between devices, shards(): lax.all_to_all(summed, 'rows', split_axis=0, concat_axis=0, tiled=True)  52.8 us
    all_to_all x1, blocking collectives, shards(): lax.all_to_all(pieces, 'rows', split_axis=0, concat_axis=0, tiled=True)  41.4 us
    another operation x14, matrix products, shards(): lower_factor = jnp.linalg.cholesky(gram_matrix)  22.9 us
    another operation x24, local copies, waits for them, and re-layouts  22.8 us
  transfers between devices with their start and end apart: 2, of which 2 were waited for; matrix products, arithmetic and copies ran while one was open for 1% of the time, Pallas kernels for 0%

commit v1 on v0

v1 whole, which is shorter than its diff:
```python
import functools
import math

import jax
import jax.numpy as jnp
import numpy as np
from jax import lax
from jax.experimental import pallas as pl
from jax.experimental.pallas import tpu as pltpu
from jax.sharding import PartitionSpec as P

FACTOR = 128
SAMPLES = 4096
COLS = 1024
ROWS_DEV = 1024
GROUP = 8
DEVICES = 128
CHIPS = 64
B = 128
NB = COLS // B
SB = 32
HALF_TILES = 20
SHARE = HALF_TILES * B // CHIPS
CHUNK = SHARE + GROUP
f32 = jnp.float32
bf16 = jnp.bfloat16
VMEM = pl.BlockSpec(memory_space=pltpu.VMEM)
SMEM = pl.BlockSpec(memory_space=pltpu.SMEM)


def tile_index(row, col):
    return row * NB - row * (row - 1) // 2 + col - row


def dg(a, b, ca, cb):
    return lax.dot_general(a, b, (((ca,), (cb,)), ((), ())), preferred_element_type=f32)


def split(x):
    high = x.astype(bf16)
    return high, (x - high.astype(f32)).astype(bf16)


def dot3(a, b, ca=1, cb=0):
    ah, al = split(a)
    bh, bl = split(b)
    return dg(ah, bh, ca, cb) + dg(ah, bl, ca, cb) + dg(al, bh, ca, cb)


def hadamard(dimension):
    positions = np.arange(dimension)
    common = positions[:, None] & positions[None, :]
    parity = np.zeros((dimension, dimension), np.int32)
    for bit in range(dimension.bit_length() - 1):
        parity ^= common >> bit & 1
    return (1 - 2 * parity).astype(np.float32)


def transform_kernel(x_ref, sign_ref, table_ref, rows_ref, out_ref):
    blocks = ROWS_DEV // FACTOR
    width = 256
    for lane in range(0, COLS, width):
        parts = []
        for b in range(blocks):
            signed = table_ref[...] * sign_ref[b : b + 1, :]
            inner = dg(signed.astype(bf16), x_ref[b * FACTOR : (b + 1) * FACTOR, lane : lane + width], 1, 0)
            parts.append(inner.astype(bf16).astype(f32))
        step = 1
        while step < blocks:
            parts = [
                parts[b] + parts[b ^ step] if not b & step else parts[b ^ step] - parts[b]
                for b in range(blocks)
            ]
            step *= 2
        for b in range(blocks):
            out_ref[b * FACTOR : (b + 1) * FACTOR, lane : lane + width] = parts[b].astype(bf16)
    for start in range(0, ROWS_DEV, 256):
        place = lax.broadcasted_iota(jnp.int32, (256, B), 0) + start
        hit = jnp.where(place == rows_ref[...], 1.0, 0.0).astype(bf16)
        ones = jnp.ones((B, B), bf16)
        out_ref[start : start + 256, COLS:] = dg(hit, ones, 1, 0).astype(bf16)


def transform(features, signs, local_rows):
    rows = jnp.concatenate([local_rows, jnp.full((B - local_rows.shape[0],), -1, jnp.int32)])[None, :]
    return pl.pallas_call(
        transform_kernel,
        out_shape=jax.ShapeDtypeStruct((ROWS_DEV, COLS + B), bf16),
        in_specs=[VMEM] * 4,
        out_specs=VMEM,
        compiler_params=pltpu.CompilerParams(vmem_limit_bytes=40 << 20),
        name="transform",
    )(features, signs.astype(f32).reshape(ROWS_DEV // FACTOR, FACTOR), jnp.asarray(hadamard(FACTOR)), rows)


def combine_kernel(core_ref, p_ref, table_ref, block_ref, mine_ref, other_ref, x_ref):
    core = core_ref[0]
    mask = p_ref[:, COLS:].astype(f32)
    row = lax.broadcasted_iota(jnp.int32, (ROWS_DEV, B), 0)
    lane = lax.broadcasted_iota(jnp.int32, (ROWS_DEV, B), 1)
    mask = jnp.where((row & (GROUP - 1)) == (lane & (GROUP - 1)), mask, 0.0).astype(bf16)
    pick = dg(block_ref[...], mask, 1, 0).astype(bf16)
    mixer = table_ref[...] * jnp.concatenate([pick] * GROUP, axis=1)
    rows = dg(mixer, p_ref[:, :COLS], 1, 0) * (1.0 / math.sqrt(SAMPLES))
    for b in range(NB):
        for half in range(2):
            x_ref[pl.ds(half * CHIPS * CHUNK + SHARE + b, CHIPS, stride=CHUNK), :] = rows[
                half * CHIPS : (half + 1) * CHIPS, b * B : (b + 1) * B
            ]
    high, low = split(rows)
    for r in range(NB):
        left_high, left_low = high[:, r * B : (r + 1) * B], low[:, r * B : (r + 1) * B]
        right_high, right_low = high[:, r * B :], low[:, r * B :]
        gram = dg(left_high, right_high, 0, 0) + dg(left_high, right_low, 0, 0) + dg(left_low, right_high, 0, 0)
        for c in range(r, NB):
            half, spot = divmod(tile_index(r, c), HALF_TILES)
            tile = gram[:, (c - r) * B : (c - r + 1) * B]
            put_rows(x_ref, half, spot * B, tile)
    for t in range(NB * (NB + 1) // 2, 2 * HALF_TILES):
        half, spot = divmod(t, HALF_TILES)
        put_rows(x_ref, half, spot * B, jnp.zeros((B, B), f32))
    size = CHIPS * CHUNK
    mine_ref[...] = x_ref[pl.ds(pl.multiple_of(core * size, 8), size), :]
    other_ref[...] = x_ref[pl.ds(pl.multiple_of((1 - core) * size, 8), size), :]


def put_rows(x_ref, half, start, tile):
    done = 0
    while done < B:
        chip, spot = divmod(start + done, SHARE)
        count = min(SHARE - spot, B - done)
        base = (half * CHIPS + chip) * CHUNK + spot
        x_ref[base : base + count, :] = tile[done : done + count, :]
        done += count


def combine(core, pieces):
    order = np.concatenate([np.arange(0, DEVICES, 2), np.arange(1, DEVICES, 2)])
    table = np.repeat(hadamard(DEVICES)[order], GROUP, axis=1)
    block = np.repeat(np.eye(DEVICES, dtype=np.float32)[order], GROUP, axis=1)
    shape = jax.ShapeDtypeStruct((CHIPS * CHUNK, B), f32)
    return pl.pallas_call(
        combine_kernel,
        out_shape=(shape, shape),
        in_specs=[SMEM, VMEM, VMEM, VMEM],
        out_specs=(VMEM, VMEM),
        scratch_shapes=[pltpu.VMEM((2 * CHIPS * CHUNK, B), f32)],
        compiler_params=pltpu.CompilerParams(vmem_limit_bytes=40 << 20),
        name="combine",
    )(core, pieces, jnp.asarray(table, bf16), jnp.asarray(block, bf16))


def factor_rows(R, lane0, w):
    rid = lax.broadcasted_iota(jnp.int32, (SB, B), 0)
    scale = jnp.ones((SB, B), f32)
    for k in range(SB):
        col = jnp.broadcast_to(R[:, lane0 + k : lane0 + k + 1], (SB, B))
        piv = col[k : k + 1, :]
        inv = 1.0 / piv
        scale = jnp.where(rid == k, jnp.broadcast_to(lax.rsqrt(piv), (SB, B)), scale)
        mult = jnp.where(rid > k, col * inv, 0.0)
        row = jnp.broadcast_to(R[k : k + 1, :], (SB, w))
        R = R - jnp.concatenate([mult] * (w // B), axis=1) * row
    return R * jnp.concatenate([scale] * (w // B), axis=1)


def factor_kernel(meta_ref, mine_ref, other_ref, rows_ref, f_ref, u_ref, lev_ref, sk_ref, a_ref, s_ref, x_ref, acc_ref):
    core = meta_ref[0]
    for k in range(SAMPLES // DEVICES):
        q = meta_ref[1 + k] // GROUP
        spot = jnp.bitwise_xor(q % 2, core)
        sk_ref[k] = rows_ref[q // 2, pl.ds(pl.multiple_of(spot * GROUP, GROUP), GROUP), :]
    first = core == 0
    for r in range(NB):
        for c in range(r, NB):
            half, spot = divmod(tile_index(r, c), HALF_TILES)
            own = mine_ref[spot * B : (spot + 1) * B, :]
            far = other_ref[spot * B : (spot + 1) * B, :]
            a_ref[r * B : (r + 1) * B, c * B : (c + 1) * B] = jnp.where(first == (half == 0), own, far)
    u_ref[...] = jnp.zeros_like(u_ref)
    x_ref[...] = jnp.zeros_like(x_ref)
    acc_ref[...] = jnp.zeros_like(acc_ref)
    ri = lax.broadcasted_iota(jnp.int32, (B, B), 0)
    ci = lax.broadcasted_iota(jnp.int32, (B, B), 1)

    def panel(p, _):
        o = pl.multiple_of(p * B, B)
        s_ref[:, :B] = a_ref[pl.ds(o, B), pl.ds(o, B)]
        s_ref[:, B:] = jnp.where(ri == ci, 1.0, 0.0).astype(f32)
        for i in range(B // SB):
            R = factor_rows(s_ref[i * SB : (i + 1) * SB, :], i * SB, 2 * B)
            s_ref[i * SB : (i + 1) * SB, :] = R
            if i < B // SB - 1:
                update = dot3(R[:, :B], R, 0, 0)
                s_ref[(i + 1) * SB :, :] = s_ref[(i + 1) * SB :, :] - update[(i + 1) * SB :, :]
        inverse = jnp.where(ri >= ci, s_ref[:, B:], 0.0)
        u_ref[pl.ds(o, B), pl.ds(o, B)] = jnp.where(ri <= ci, s_ref[:, :B], 0.0)

        def across(q, _):
            oq = pl.multiple_of(q * B, B)
            u_ref[pl.ds(o, B), pl.ds(oq, B)] = dot3(inverse, a_ref[pl.ds(o, B), pl.ds(oq, B)])
            return 0

        lax.fori_loop(p + 1, NB, across, 0)

        def trail(q, _):
            oq = pl.multiple_of(q * B, B)
            a_ref[pl.ds(oq, B), :] = a_ref[pl.ds(oq, B), :] - dot3(u_ref[pl.ds(o, B), pl.ds(oq, B)], u_ref[pl.ds(o, B), :], 0, 0)
            return 0

        lax.fori_loop(p + 1, NB, trail, 0)
        above = lax.broadcasted_iota(jnp.int32, (COLS, B), 0) < o
        ucol = jnp.where(above, u_ref[:, pl.ds(o, B)], 0.0)
        x_ref[:, pl.ds(o, B)] = -dot3(dot3(x_ref[...], ucol), inverse, 1, 1)
        x_ref[pl.ds(o, B), pl.ds(o, B)] = inverse.T
        high, low = split(x_ref[:, pl.ds(o, B)])
        w = dg(f_ref[...], high, 1, 0) + dg(f_ref[...], low, 1, 0)
        acc_ref[...] += w * w
        return 0

    lax.fori_loop(0, NB, panel, 0)
    lev_ref[...] = lax.dot_general(
        jnp.full((8, B), float(DEVICES * ROWS_DEV // COLS), f32),
        acc_ref[...],
        (((1,), (1,)), ((), ())),
        precision=lax.Precision.HIGHEST,
        preferred_element_type=f32,
    )


def factor(meta, mine, other, rows, features):
    return pl.pallas_call(
        factor_kernel,
        out_shape=(
            jax.ShapeDtypeStruct((COLS, COLS), f32),
            jax.ShapeDtypeStruct((8, ROWS_DEV), f32),
            jax.ShapeDtypeStruct((SAMPLES // DEVICES, GROUP, B), f32),
        ),
        in_specs=[SMEM] + [VMEM] * 4,
        out_specs=(VMEM,) * 3,
        scratch_shapes=[
            pltpu.VMEM((COLS, COLS), f32),
            pltpu.VMEM((B, 2 * B), f32),
            pltpu.VMEM((COLS, COLS), f32),
            pltpu.VMEM((ROWS_DEV, B), f32),
        ],
        compiler_params=pltpu.CompilerParams(vmem_limit_bytes=60 << 20),
        name="factor",
    )(meta, mine, other, rows, features)


def shards(features, flip_signs, sample_rows):
    position = lax.axis_index("rows")
    core = position % 2
    local_rows = sample_rows - position * ROWS_DEV
    mixed = transform(features, flip_signs, local_rows)
    pieces = lax.all_to_all(
        mixed.reshape(DEVICES, GROUP, COLS + B), "rows", split_axis=0, concat_axis=0, tiled=True
    ).reshape(ROWS_DEV, COLS + B)
    mine, other = combine(core[None], pieces)
    swap = [(d, d ^ 1) for d in range(DEVICES)]
    came = lax.ppermute(other, "rows", swap).reshape(CHIPS, CHUNK, B)
    mine = mine.reshape(CHIPS, CHUNK, B)
    shares = jnp.concatenate([mine[:, :SHARE] + came[:, :SHARE], mine[:, SHARE:], came[:, SHARE:]], axis=1)
    same_core = [list(range(c, DEVICES, 2)) for c in range(2)]
    got = lax.all_to_all(
        shares, "rows", split_axis=0, concat_axis=0, tiled=True, axis_index_groups=same_core
    )
    total = jnp.sum(got[:, :SHARE], axis=0)
    half = lax.all_to_all(
        jnp.broadcast_to(total[None], (CHIPS, SHARE, B)),
        "rows", split_axis=0, concat_axis=0, tiled=True, axis_index_groups=same_core,
    ).reshape(HALF_TILES * B, B)
    far = lax.ppermute(half, "rows", swap)
    meta = jnp.concatenate([core[None], local_rows])
    upper, lev, sketch = factor(meta, half, far, got[:, SHARE:], features)
    return sketch.reshape(-1, COLS), upper, lev[0]


def solution(mesh):
    placed = (P("rows", None), P("rows"), P("rows"))
    return jax.shard_map(
        shards,
        mesh=mesh,
        in_specs=placed,
        out_specs=(P("rows", None), P(), P("rows")),
        check_vma=False,
    )
```

time: 634 us -> 280 us (0.44); the launches traced: 625 us -> 280 us
  other arithmetic: 269 us -> 2.33 us
  Pallas kernels: 0 us -> 160 us
  matrix products: 113 us -> 0 us
  waiting for transfers between devices: 124 us -> 37.2 us
  local copies, waits for them, and re-layouts: 52.3 us -> 8.82 us
  between operations: 19.6 us -> 0.72 us
  blocking collectives: 41.4 us -> 54.6 us
  starting transfers between devices: 6.02 us -> 16.3 us
    another operation x33 -> x0, other arithmetic: 258 us -> none  [the longest x30 172 us: shards(): lower_factor = jnp.linalg.cholesky(gram_matrix)]
    pallas_call x0 -> x3, Pallas kernels: none -> 160 us  [the longest x1 157 us: factor(): pl.pallas_call(factor_kernel, out_shape=(jax.ShapeDtypeStruct((COLS, COLS...]
    all_gather x1 -> x0, waiting for transfers between devices: 70.8 us -> none  [shards(): all_rows = lax.all_gather(sketch, 'rows', axis=0, tiled=True)]
    dot_general x4 -> x0, matrix products: 67.9 us -> none  [the longest x1 62 us: shards(): gram_matrix = jnp.dot(all_rows.T, all_rows, precision=lax.Precision.HIGHEST)]
    another operation x29 -> x0, matrix products: 44.8 us -> none  [the longest x14 22.9 us: shards(): lower_factor = jnp.linalg.cholesky(gram_matrix)]
    another operation x33 -> x0, local copies, waits for them, and re-layouts: 25.4 us -> none
    all_to_all x1, waiting for transfers between devices: 52.8 us -> 32.9 us  [shards(): lax.all_to_all(mixed.reshape(DEVICES, GROUP, COLS + B), 'rows', split_axi...]
    all_to_all x1 -> x2, blocking collectives: 41.4 us -> 54.6 us  [the longest x1 29.8 us: shards(): lax.all_to_all(shares, 'rows', split_axis=0, concat_axis=0, tiled=True, a...]
  transfers between devices with their start and end apart: 2 -> 3, of which waited for: 2 -> 3; matrix products, arithmetic and copies ran while one was open for 1% -> 1% of each run, Pallas kernels for 0% -> 0%
where the time goes in v1:
time: 280 us
  Pallas kernels  160 us (57%)
  blocking collectives  54.6 us (20%)
  waiting for transfers between devices  37.2 us (13%)
  starting transfers between devices  16.3 us (6%)
  local copies, waits for them, and re-layouts  8.82 us (3%)
    pallas_call x1, Pallas kernels, factor(): pl.pallas_call(factor_kernel, out_shape=(jax.ShapeDtypeStruct((COLS, COLS...  157 us
    all_to_all x1, waiting for transfers between devices, shards(): lax.all_to_all(mixed.reshape(DEVICES, GROUP, COLS + B), 'rows', split_axi...  32.9 us
    all_to_all x1, blocking collectives, shards(): lax.all_to_all(shares, 'rows', split_axis=0, concat_axis=0, tiled=True, a...  29.8 us
    all_to_all x1, blocking collectives, shards(): lax.all_to_all(jnp.broadcast_to(total[None], (CHIPS, SHARE, B)), 'rows',...  24.8 us
    all_to_all x1, starting transfers between devices, shards(): lax.all_to_all(mixed.reshape(DEVICES, GROUP, COLS + B), 'rows', split_axi...  11.5 us
    unnamed x15, local copies, waits for them, and re-layouts  6.49 us
  transfers between devices with their start and end apart: 3, of which 3 were waited for; matrix products, arithmetic and copies ran while one was open for 1% of the time, Pallas kernels for 0%

profile of v1, /device:TPU:1, one launch (start us, length us, event | category | flops | bytes accessed | tf_op | source)
XLA Modules:
  0.0 279.9 jit_solution(14126675343330160156)
XLA Ops:
  0.6 0.7 broadcast_subtract_fusion
  1.3 0.7 convert_bitcast_fusion.sign_ref
  2.0 0.0 copy-start.1
  2.0 1.6 copy-done.1
  3.6 0.0 copy-start.4
  3.6 0.8 copy-done.4
  4.4 1.3 transform.1
  5.7 0.0 copy-start
  5.7 1.4 copy-done
  7.1 0.0 copy-start.2
  7.1 11.5 %all-to-all-start = ((bf16[128,8,1152]{2,1,0:T(8,128)(2,1)}), bf16[128,8,1152]{2,1,0:T(8,128)(2,1)S(1)}, u32[]{:S(2)}, u32[]{:S(2)}) async-start(bf16[128,8,1152]{2,1,0:T(8,128)(2,1)} %bitcast.16), calls=%async_computation | async-start | bytes 4718592 | tf_op jit(solution)/shard_map/all_to_all | solution.py:257
  18.6 32.9 %all-to-all-done = bf16[128,8,1152]{2,1,0:T(8,128)(2,1)S(1)} async-done(((bf16[128,8,1152]{2,1,0:T(8,128)(2,1)}), bf16[128,8,1152]{2,1,0:T(8,128)(2,1)S(1)}, u32[]{:S(2)}, u32[]{:S(2)}) %all-to-all-start) | async-done | bytes 2359328 | tf_op jit(solution)/shard_map/all_to_all | solution.py:257
  51.6 0.0 copy-done.2
  51.6 0.0 copy-done.3
  51.6 2.0 combine.1
  53.5 1.4 collective-permute-start
  54.9 3.0 %collective-permute-done = f32[3072,128]{1,0:T(8,128)S(1)} collective-permute-done((f32[3072,128]{1,0:T(8,128)S(1)}, f32[3072,128]{1,0:T(8,128)S(1)}, u32[]{:S(2)}, u32[]{:S(2)}) %collective-permute-start) | collective-permute-done | bytes 1572896 | tf_op jit(solution)/shard_map/ppermute | solution.py:262
  57.9 0.2 slice_add_fusion
  58.1 0.1 pad_maximum_fusion
  58.3 29.8 %all_to_all.15 = f32[64,56,128]{2,1,0:T(8,128)S(1)} all-to-all(f32[64,56,128]{2,1,0:T(8,128)S(1)} %pad_maximum_fusion), channel_id=1, replica_groups={{0,2,4,6,8,10,12,14,16,18,20,22,24,26,28,30,32,34,36,38,40,42,44,46,48,..., dimensions={0} | all-to-all | bytes 3670016 | tf_op jit(solution)/shard_map/all_to_all | solution.py:266
  88.1 0.1 slice_reduce_fusion
  88.2 0.1 broadcast_in_dim.16
  88.3 24.8 %all_to_all.16 = f32[64,40,128]{2,1,0:T(8,128)S(1)} all-to-all(f32[64,40,128]{2,1,0:T(8,128)S(1)} %broadcast_in_dim.16), channel_id=1, replica_groups={{0,2,4,6,8,10,12,14,16,18,20,22,24,26,28,30,32,34,36,38,40,42,44,46,48,..., dimensions={0} | all-to-all | bytes 2621440 | tf_op jit(solution)/shard_map/all_to_all | solution.py:270
  113.0 3.5 %collective-permute-start.1 = (f32[2560,128]{1,0:T(8,128)S(1)}, f32[2560,128]{1,0:T(8,128)S(1)}, u32[]{:S(2)}, u32[]{:S(2)}) collective-permute-start(f32[2560,128]{1,0:T(8,128)S(1)} %bitcast.19), channel_id=1, source_target_pairs={{0,1},{1,0},{2,3},{3,2},{4,5},{5,4},{6,7},{7,6},{8,9},{9,8},{10,11... | collective-permute-start | bytes 3932168 | tf_op jit(solution)/shard_map/ppermute | solution.py:274
  116.5 0.6 pad_add_fusion.meta_ref
  117.1 0.8 slice.33.rows_ref
  117.9 1.2 collective-permute-done.1.other_ref
  119.2 0.0 copy-done.5
  119.2 1.1 copy-done.6
  120.3 156.7 %factor.1 = (f32[1024,1024]{1,0:T(8,128)}, f32[8,1024]{1,0:T(8,128)}, f32[32,8,128]{2,1,0:T(8,128)}) custom-call(s32[33]{0:T(128)} %pad_add_fusion.meta_ref, f32[2560,128]{1,0:T(8,128)} %bitcast.20, f32[2560,128]{1,0:T(8,128)} %copy-done.6, f32[64,16,128]{2,1,0:T(8,128)} %slice.33.rows_ref, bf16[1024,1024]{1,0:T(8,128)(2,1)} %f_ref.1), custom_call_target="tpu_custom_call" | custom-call | tf_op jit(solution)/shard_map/factor/pallas_call | solution.py:232
  277.0 1.6 copy.11
  278.6 1.4 slice.27
  (6 shorter events, 0.0 us)
Async XLA Ops:
  2.0 1.6 copy-start.1
  3.6 0.8 copy-start.4
  5.7 1.4 copy-start
  7.1 44.4 %copy-start.2 = (bf16[128,1024]{1,0:T(8,128)(2,1)S(1)}, bf16[128,1024]{1,0:T(8,128)(2,1)}, u32[]{:S(2)}) copy-start(bf16[128,1024]{1,0:T(8,128)(2,1)} %constant.31.clone.block_ref) | copy-start | bytes 786436
  7.1 44.4 %copy-start.3 = (bf16[128,1024]{1,0:T(8,128)(2,1)S(1)}, bf16[128,1024]{1,0:T(8,128)(2,1)}, u32[]{:S(2)}) copy-start(bf16[128,1024]{1,0:T(8,128)(2,1)} %constant.30.clone.table_ref) | copy-start | bytes 786436
  7.1 44.4 %all-to-all-start = ((bf16[128,8,1152]{2,1,0:T(8,128)(2,1)}), bf16[128,8,1152]{2,1,0:T(8,128)(2,1)S(1)}, u32[]{:S(2)}, u32[]{:S(2)}) async-start(bf16[128,8,1152]{2,1,0:T(8,128)(2,1)} %bitcast.16), calls=%async_computation | async-start | bytes 4718592 | tf_op jit(solution)/shard_map/all_to_all | solution.py:257
  53.5 4.4 %collective-permute-start = (f32[3072,128]{1,0:T(8,128)S(1)}, f32[3072,128]{1,0:T(8,128)S(1)}, u32[]{:S(2)}, u32[]{:S(2)}) collective-permute-start(f32[3072,128]{1,0:T(8,128)S(1)} %get-tuple-element.9), channel_id=1, source_target_pairs={{0,1},{1,0},{2,3},{3,2},{4,5},{5,4},{6,7},{7,6},{8,9},{9,8},{10,11... | collective-permute-start | bytes 4718600 | tf_op jit(solution)/shard_map/ppermute | solution.py:262
  113.0 6.1 %copy-start.5 = (f32[64,40,128]{2,1,0:T(8,128)}, f32[64,40,128]{2,1,0:T(8,128)S(1)}, u32[]{:S(2)}) copy-start(f32[64,40,128]{2,1,0:T(8,128)S(1)} %all_to_all.16) | copy-start | bytes 3932164
  113.0 6.1 %collective-permute-start.1 = (f32[2560,128]{1,0:T(8,128)S(1)}, f32[2560,128]{1,0:T(8,128)S(1)}, u32[]{:S(2)}, u32[]{:S(2)}) collective-permute-start(f32[2560,128]{1,0:T(8,128)S(1)} %bitcast.19), channel_id=1, source_target_pairs={{0,1},{1,0},{2,3},{3,2},{4,5},{5,4},{6,7},{7,6},{8,9},{9,8},{10,11... | collective-permute-start | bytes 3932168 | tf_op jit(solution)/shard_map/ppermute | solution.py:274
  119.2 1.1 copy-start.6

commit v2 on v1

--- a/solution.py
+++ b/solution.py
@@ -1,4 +1,3 @@
-import functools
 import math
 
 import jax
@@ -41,10 +40,13 @@
     return high, (x - high.astype(f32)).astype(bf16)
 
 
+def dot3s(a, b, ca=1, cb=0):
+    (ah, al), (bh, bl) = a, b
+    return dg(ah, bh, ca, cb) + dg(ah, bl, ca, cb) + dg(al, bh, ca, cb)
+
+
 def dot3(a, b, ca=1, cb=0):
-    ah, al = split(a)
-    bh, bl = split(b)
-    return dg(ah, bh, ca, cb) + dg(ah, bl, ca, cb) + dg(al, bh, ca, cb)
+    return dot3s(split(a), split(b), ca, cb)
 
 
 def hadamard(dimension):
@@ -150,21 +152,78 @@
     )(core, pieces, jnp.asarray(table, bf16), jnp.asarray(block, bf16))
 
 
-def factor_rows(R, lane0, w):
-    rid = lax.broadcasted_iota(jnp.int32, (SB, B), 0)
-    scale = jnp.ones((SB, B), f32)
-    for k in range(SB):
-        col = jnp.broadcast_to(R[:, lane0 + k : lane0 + k + 1], (SB, B))
-        piv = col[k : k + 1, :]
-        inv = 1.0 / piv
-        scale = jnp.where(rid == k, jnp.broadcast_to(lax.rsqrt(piv), (SB, B)), scale)
-        mult = jnp.where(rid > k, col * inv, 0.0)
-        row = jnp.broadcast_to(R[k : k + 1, :], (SB, w))
-        R = R - jnp.concatenate([mult] * (w // B), axis=1) * row
-    return R * jnp.concatenate([scale] * (w // B), axis=1)
-
-
-def factor_kernel(meta_ref, mine_ref, other_ref, rows_ref, f_ref, u_ref, lev_ref, sk_ref, a_ref, s_ref, x_ref, acc_ref):
+def factor_rows(s_ref, i):
+    groups = SB // 8
+    rid = lax.broadcasted_iota(jnp.int32, (8, B), 0)
+    base = i * SB
+    R = [[s_ref[base + 8 * v : base + 8 * v + 8, h * B : (h + 1) * B] for h in range(2)] for v in range(groups)]
+
+    def spread(x, k):
+        return jnp.broadcast_to(x[k : k + 1, :], (8, B))
+
+    for g in range(groups):
+        lane = base + 8 * g
+        rest = range(groups - g)
+        C = [[jnp.broadcast_to(R[g + v][0][:, lane + k : lane + k + 1], (8, B)) for v in rest] for k in range(8)]
+        scale = None
+        for k in range(8):
+            pivot = spread(C[k][0], k)
+            inverse = 1.0 / pivot
+            factors = [C[k][v] * inverse for v in rest]
+            factors[0] = jnp.where(rid > k, factors[0], 0.0)
+            for j in range(k + 1, 8):
+                row = spread(C[j][0], k)
+                for v in rest:
+                    C[j][v] = C[j][v] - factors[v] * row
+            for h in range(2):
+                row = spread(R[g][h], k)
+                for v in rest:
+                    R[g + v][h] = R[g + v][h] - factors[v] * row
+            root = lax.rsqrt(pivot)
+            scale = root if scale is None else jnp.where(rid >= k, root, scale)
+        for h in range(2):
+            R[g][h] = R[g][h] * scale
+    for v in range(groups):
+        for h in range(2):
+            s_ref[base + 8 * v : base + 8 * v + 8, h * B : (h + 1) * B] = R[v][h]
+
+
+def finish_panel(p, f_ref, u_ref, a_ref, s_ref, uh_ref, ul_ref, xh_ref, xl_ref, acc_ref):
+    o = p * B
+    e = o + B
+    ri = lax.broadcasted_iota(jnp.int32, (B, B), 0)
+    ci = lax.broadcasted_iota(jnp.int32, (B, B), 1)
+    inverse = jnp.where(ri >= ci, s_ref[:, B:], 0.0)
+    u_ref[o:e, o:e] = jnp.where(ri <= ci, s_ref[:, :B], 0.0)
+    if e < COLS:
+        across = dot3s(split(inverse), split(a_ref[o:e, e:]))
+        u_ref[o:e, e:] = across
+        high, low = split(across)
+        uh_ref[o:e, e:] = high
+        ul_ref[o:e, e:] = low
+        for q in range(p + 1, NB):
+            c = q * B - e
+            left = jnp.concatenate([high[:, c : c + B], high[:, c : c + B], low[:, c : c + B]], axis=0)
+            right = jnp.concatenate([high[:, c:], low[:, c:], high[:, c:]], axis=0)
+            a_ref[q * B : (q + 1) * B, q * B :] -= dg(left, right, 0, 0)
+    corner = split(inverse.T)
+    if p > 0:
+        above = dot3s((xh_ref[:o, :o], xl_ref[:o, :o]), (uh_ref[:o, o:e], ul_ref[:o, o:e]))
+        xh_ref[:o, o:e], xl_ref[:o, o:e] = split(-dot3s(split(above), corner))
+    xh_ref[o:e, o:e], xl_ref[o:e, o:e] = corner
+    if e < COLS:
+        xh_ref[e:, o:e] = jnp.zeros((COLS - e, B), bf16)
+        xl_ref[e:, o:e] = jnp.zeros((COLS - e, B), bf16)
+    if p % 2:
+        pair = slice(o - B, e)
+        w = dg(f_ref[:, :e], xh_ref[:e, pair], 1, 0) + dg(f_ref[:, :e], xl_ref[:e, pair], 1, 0)
+        acc_ref[...] += w * w
+
+
+def factor_kernel(
+    meta_ref, mine_ref, other_ref, rows_ref, f_ref, u_ref, lev_ref, sk_ref,
+    a_ref, s_ref, uh_ref, ul_ref, xh_ref, xl_ref, acc_ref,
+):
     core = meta_ref[0]
     for k in range(SAMPLES // DEVICES):
         q = meta_ref[1 + k] // GROUP
@@ -178,7 +237,6 @@
             far = other_ref[spot * B : (spot + 1) * B, :]
             a_ref[r * B : (r + 1) * B, c * B : (c + 1) * B] = jnp.where(first == (half == 0), own, far)
     u_ref[...] = jnp.zeros_like(u_ref)
-    x_ref[...] = jnp.zeros_like(x_ref)
     acc_ref[...] = jnp.zeros_like(acc_ref)
     ri = lax.broadcasted_iota(jnp.int32, (B, B), 0)
     ci = lax.broadcasted_iota(jnp.int32, (B, B), 1)
@@ -188,44 +246,23 @@
         s_ref[:, :B] = a_ref[pl.ds(o, B), pl.ds(o, B)]
         s_ref[:, B:] = jnp.where(ri == ci, 1.0, 0.0).astype(f32)
         for i in range(B // SB):
-            R = factor_rows(s_ref[i * SB : (i + 1) * SB, :], i * SB, 2 * B)
-            s_ref[i * SB : (i + 1) * SB, :] = R
+            factor_rows(s_ref, i)
             if i < B // SB - 1:
+                R = s_ref[i * SB : (i + 1) * SB, :]
                 update = dot3(R[:, :B], R, 0, 0)
                 s_ref[(i + 1) * SB :, :] = s_ref[(i + 1) * SB :, :] - update[(i + 1) * SB :, :]
-        inverse = jnp.where(ri >= ci, s_ref[:, B:], 0.0)
-        u_ref[pl.ds(o, B), pl.ds(o, B)] = jnp.where(ri <= ci, s_ref[:, :B], 0.0)
-
-        def across(q, _):
-            oq = pl.multiple_of(q * B, B)
-            u_ref[pl.ds(o, B), pl.ds(oq, B)] = dot3(inverse, a_ref[pl.ds(o, B), pl.ds(oq, B)])
-            return 0
-
-        lax.fori_loop(p + 1, NB, across, 0)
-
-        def trail(q, _):
-            oq = pl.multiple_of(q * B, B)
-            a_ref[pl.ds(oq, B), :] = a_ref[pl.ds(oq, B), :] - dot3(u_ref[pl.ds(o, B), pl.ds(oq, B)], u_ref[pl.ds(o, B), :], 0, 0)
-            return 0
-
-        lax.fori_loop(p + 1, NB, trail, 0)
-        above = lax.broadcasted_iota(jnp.int32, (COLS, B), 0) < o
-        ucol = jnp.where(above, u_ref[:, pl.ds(o, B)], 0.0)
-        x_ref[:, pl.ds(o, B)] = -dot3(dot3(x_ref[...], ucol), inverse, 1, 1)
-        x_ref[pl.ds(o, B), pl.ds(o, B)] = inverse.T
-        high, low = split(x_ref[:, pl.ds(o, B)])
-        w = dg(f_ref[...], high, 1, 0) + dg(f_ref[...], low, 1, 0)
-        acc_ref[...] += w * w
+        for static in range(NB):
+
+            @pl.when(p == static)
+            def _():
+                finish_panel(static, f_ref, u_ref, a_ref, s_ref, uh_ref, ul_ref, xh_ref, xl_ref, acc_ref)
+
         return 0
 
     lax.fori_loop(0, NB, panel, 0)
-    lev_ref[...] = lax.dot_general(
-        jnp.full((8, B), float(DEVICES * ROWS_DEV // COLS), f32),
-        acc_ref[...],
-        (((1,), (1,)), ((), ())),
-        precision=lax.Precision.HIGHEST,
-        preferred_element_type=f32,
-    )
+    high, low = split(acc_ref[...])
+    weight = jnp.full((8, 2 * B), float(DEVICES * ROWS_DEV // COLS), bf16)
+    lev_ref[...] = dg(weight, high, 1, 1) + dg(weight, low, 1, 1)
 
 
 def factor(meta, mine, other, rows, features):
@@ -238,12 +275,9 @@
         ),
         in_specs=[SMEM] + [VMEM] * 4,
         out_specs=(VMEM,) * 3,
-        scratch_shapes=[
-            pltpu.VMEM((COLS, COLS), f32),
-            pltpu.VMEM((B, 2 * B), f32),
-            pltpu.VMEM((COLS, COLS), f32),
-            pltpu.VMEM((ROWS_DEV, B), f32),
-        ],
+        scratch_shapes=[pltpu.VMEM((COLS, COLS), f32), pltpu.VMEM((B, 2 * B), f32)]
+        + [pltpu.VMEM((COLS, COLS), bf16)] * 4
+        + [pltpu.VMEM((ROWS_DEV, 2 * B), f32)],
         compiler_params=pltpu.CompilerParams(vmem_limit_bytes=60 << 20),
         name="factor",
     )(meta, mine, other, rows, features)

time: 280 us -> 175 us (0.62)
  Pallas kernels: 160 us -> 54.9 us
    pallas_call x1, Pallas kernels: 157 us -> 51.6 us  [factor(): pl.pallas_call(factor_kernel, out_shape=(jax.ShapeDtypeStruct((COLS, COLS...]
where the time goes in v2:
time: 175 us
  Pallas kernels  54.9 us (31%)
  blocking collectives  54.6 us (31%)
  waiting for transfers between devices  37.2 us (21%)
  starting transfers between devices  16.3 us (9%)
  local copies, waits for them, and re-layouts  8.82 us (5%)
  other arithmetic  2.33 us (1%)
    pallas_call x1, Pallas kernels, factor(): pl.pallas_call(factor_kernel, out_shape=(jax.ShapeDtypeStruct((COLS, COLS...  51.6 us
    all_to_all x1, waiting for transfers between devices, shards(): lax.all_to_all(mixed.reshape(DEVICES, GROUP, COLS + B), 'rows', split_axi...  32.9 us
    all_to_all x1, blocking collectives, shards(): lax.all_to_all(shares, 'rows', split_axis=0, concat_axis=0, tiled=True, a...  29.8 us
    all_to_all x1, blocking collectives, shards(): lax.all_to_all(jnp.broadcast_to(total[None], (CHIPS, SHARE, B)), 'rows',...  24.8 us
    all_to_all x1, starting transfers between devices, shards(): lax.all_to_all(mixed.reshape(DEVICES, GROUP, COLS + B), 'rows', split_axi...  11.5 us
    unnamed x15, local copies, waits for them, and re-layouts  6.49 us
  transfers between devices with their start and end apart: 3, of which 3 were waited for; matrix products, arithmetic and copies ran while one was open for 1% of the time, Pallas kernels for 0%

profile of v2, /device:TPU:1, one launch (start us, length us, event | category | flops | bytes accessed | tf_op | source)
XLA Modules:
  0.0 174.8 jit_solution(14557567340843239736)
XLA Ops:
  0.6 0.7 broadcast_subtract_fusion
  1.3 0.7 convert_bitcast_fusion.sign_ref
  2.0 0.0 copy-start.1
  2.0 1.6 copy-done.1
  3.6 0.0 copy-start.4
  3.6 0.8 copy-done.4
  4.4 1.3 transform.1
  5.7 0.0 copy-start
  5.7 1.4 copy-done
  7.1 0.0 copy-start.2
  7.1 11.5 %all-to-all-start = ((bf16[128,8,1152]{2,1,0:T(8,128)(2,1)}), bf16[128,8,1152]{2,1,0:T(8,128)(2,1)S(1)}, u32[]{:S(2)}, u32[]{:S(2)}) async-start(bf16[128,8,1152]{2,1,0:T(8,128)(2,1)} %bitcast.16), calls=%async_computation | async-start | bytes 4718592 | tf_op jit(solution)/shard_map/all_to_all | solution.py:291
  18.6 32.9 %all-to-all-done = bf16[128,8,1152]{2,1,0:T(8,128)(2,1)S(1)} async-done(((bf16[128,8,1152]{2,1,0:T(8,128)(2,1)}), bf16[128,8,1152]{2,1,0:T(8,128)(2,1)S(1)}, u32[]{:S(2)}, u32[]{:S(2)}) %all-to-all-start) | async-done | bytes 2359328 | tf_op jit(solution)/shard_map/all_to_all | solution.py:291
  51.6 0.0 copy-done.2
  51.6 0.0 copy-done.3
  51.6 2.0 %combine.1 = (f32[3072,128]{1,0:T(8,128)S(1)}, f32[3072,128]{1,0:T(8,128)S(1)}) custom-call(s32[1]{0:T(128)} %bitcast.core_ref, bf16[1024,1152]{1,0:T(8,128)(2,1)S(1)} %bitcast.15, bf16[128,1024]{1,0:T(8,128)(2,1)S(1)} %copy-done.3, bf16[128,1024]{1,0:T(8,128)(2,1)S(1)} %copy-done.2), custom_call_target="tpu_custom_call" | custom-call | tf_op jit(solution)/shard_map/combine/pallas_call | solution.py:144
  53.5 1.4 collective-permute-start
  54.9 3.0 %collective-permute-done = f32[3072,128]{1,0:T(8,128)S(1)} collective-permute-done((f32[3072,128]{1,0:T(8,128)S(1)}, f32[3072,128]{1,0:T(8,128)S(1)}, u32[]{:S(2)}, u32[]{:S(2)}) %collective-permute-start) | collective-permute-done | bytes 1572896 | tf_op jit(solution)/shard_map/ppermute | solution.py:296
  57.9 0.2 slice_add_fusion
  58.1 0.1 pad_maximum_fusion
  58.3 29.8 %all_to_all.15 = f32[64,56,128]{2,1,0:T(8,128)S(1)} all-to-all(f32[64,56,128]{2,1,0:T(8,128)S(1)} %pad_maximum_fusion), channel_id=1, replica_groups={{0,2,4,6,8,10,12,14,16,18,20,22,24,26,28,30,32,34,36,38,40,42,44,46,48,..., dimensions={0} | all-to-all | bytes 3670016 | tf_op jit(solution)/shard_map/all_to_all | solution.py:300
  88.1 0.1 slice_reduce_fusion
  88.2 0.1 broadcast_in_dim.16
  88.3 24.8 %all_to_all.16 = f32[64,40,128]{2,1,0:T(8,128)S(1)} all-to-all(f32[64,40,128]{2,1,0:T(8,128)S(1)} %broadcast_in_dim.16), channel_id=1, replica_groups={{0,2,4,6,8,10,12,14,16,18,20,22,24,26,28,30,32,34,36,38,40,42,44,46,48,..., dimensions={0} | all-to-all | bytes 2621440 | tf_op jit(solution)/shard_map/all_to_all | solution.py:304
  113.0 3.5 %collective-permute-start.1 = (f32[2560,128]{1,0:T(8,128)S(1)}, f32[2560,128]{1,0:T(8,128)S(1)}, u32[]{:S(2)}, u32[]{:S(2)}) collective-permute-start(f32[2560,128]{1,0:T(8,128)S(1)} %bitcast.19), channel_id=1, source_target_pairs={{0,1},{1,0},{2,3},{3,2},{4,5},{5,4},{6,7},{7,6},{8,9},{9,8},{10,11... | collective-permute-start | bytes 3932168 | tf_op jit(solution)/shard_map/ppermute | solution.py:308
  116.5 0.6 pad_add_fusion.meta_ref
  117.1 0.8 slice.33.rows_ref
  117.9 1.2 collective-permute-done.1.other_ref
  119.2 0.0 copy-done.5
  119.2 1.1 copy-done.6
  120.3 51.6 %factor.1 = (f32[1024,1024]{1,0:T(8,128)}, f32[8,1024]{1,0:T(8,128)}, f32[32,8,128]{2,1,0:T(8,128)}) custom-call(s32[33]{0:T(128)} %pad_add_fusion.meta_ref, f32[2560,128]{1,0:T(8,128)} %bitcast.20, f32[2560,128]{1,0:T(8,128)} %copy-done.6, f32[64,16,128]{2,1,0:T(8,128)} %slice.33.rows_ref, bf16[1024,1024]{1,0:T(8,128)(2,1)} %f_ref.1), custom_call_target="tpu_custom_call" | custom-call | tf_op jit(solution)/shard_map/factor/pallas_call | solution.py:269
  171.8 1.6 copy.11
  173.4 1.4 slice.27
  (6 shorter events, 0.0 us)
Async XLA Ops:
  2.0 1.6 copy-start.1
  3.6 0.8 copy-start.4
  5.7 1.4 copy-start
  7.1 44.4 %copy-start.2 = (bf16[128,1024]{1,0:T(8,128)(2,1)S(1)}, bf16[128,1024]{1,0:T(8,128)(2,1)}, u32[]{:S(2)}) copy-start(bf16[128,1024]{1,0:T(8,128)(2,1)} %constant.31.clone.block_ref) | copy-start | bytes 786436
  7.1 44.4 %copy-start.3 = (bf16[128,1024]{1,0:T(8,128)(2,1)S(1)}, bf16[128,1024]{1,0:T(8,128)(2,1)}, u32[]{:S(2)}) copy-start(bf16[128,1024]{1,0:T(8,128)(2,1)} %constant.30.clone.table_ref) | copy-start | bytes 786436
  7.1 44.4 %all-to-all-start = ((bf16[128,8,1152]{2,1,0:T(8,128)(2,1)}), bf16[128,8,1152]{2,1,0:T(8,128)(2,1)S(1)}, u32[]{:S(2)}, u32[]{:S(2)}) async-start(bf16[128,8,1152]{2,1,0:T(8,128)(2,1)} %bitcast.16), calls=%async_computation | async-start | bytes 4718592 | tf_op jit(solution)/shard_map/all_to_all | solution.py:291
  53.5 4.4 %collective-permute-start = (f32[3072,128]{1,0:T(8,128)S(1)}, f32[3072,128]{1,0:T(8,128)S(1)}, u32[]{:S(2)}, u32[]{:S(2)}) collective-permute-start(f32[3072,128]{1,0:T(8,128)S(1)} %get-tuple-element.9), channel_id=1, source_target_pairs={{0,1},{1,0},{2,3},{3,2},{4,5},{5,4},{6,7},{7,6},{8,9},{9,8},{10,11... | collective-permute-start | bytes 4718600 | tf_op jit(solution)/shard_map/ppermute | solution.py:296
  113.0 6.1 %copy-start.5 = (f32[64,40,128]{2,1,0:T(8,128)}, f32[64,40,128]{2,1,0:T(8,128)S(1)}, u32[]{:S(2)}) copy-start(f32[64,40,128]{2,1,0:T(8,128)S(1)} %all_to_all.16) | copy-start | bytes 3932164
  113.0 6.1 %collective-permute-start.1 = (f32[2560,128]{1,0:T(8,128)S(1)}, f32[2560,128]{1,0:T(8,128)S(1)}, u32[]{:S(2)}, u32[]{:S(2)}) collective-permute-start(f32[2560,128]{1,0:T(8,128)S(1)} %bitcast.19), channel_id=1, source_target_pairs={{0,1},{1,0},{2,3},{3,2},{4,5},{5,4},{6,7},{7,6},{8,9},{9,8},{10,11... | collective-permute-start | bytes 3932168 | tf_op jit(solution)/shard_map/ppermute | solution.py:308
  119.2 1.1 copy-start.6

commit v3 on v2

--- a/solution.py
+++ b/solution.py
@@ -23,6 +23,7 @@
 CHUNK = SHARE + GROUP
 f32 = jnp.float32
 bf16 = jnp.bfloat16
+ANY = pl.BlockSpec(memory_space=pl.ANY)
 VMEM = pl.BlockSpec(memory_space=pltpu.VMEM)
 SMEM = pl.BlockSpec(memory_space=pltpu.SMEM)
 
@@ -58,45 +59,76 @@
     return (1 - 2 * parity).astype(np.float32)
 
 
-def transform_kernel(x_ref, sign_ref, table_ref, rows_ref, out_ref):
+def transform_kernel(x_hbm, sign_ref, rows_ref, table_ref, out_hbm, x_ref, out_ref, in_sem, out_sem):
     blocks = ROWS_DEV // FACTOR
     width = 256
-    for lane in range(0, COLS, width):
-        parts = []
+    parts = COLS // width
+
+    def fetch(c):
+        lanes = pl.ds(c * width, width)
+        return pltpu.make_async_copy(x_hbm.at[:, lanes], x_ref.at[:, lanes], in_sem.at[c])
+
+    def put(c):
+        lanes = pl.ds(c * width, width) if c < parts else pl.ds(COLS, B)
+        return pltpu.make_async_copy(out_ref.at[:, lanes], out_hbm.at[:, lanes], out_sem.at[c])
+
+    for c in range(parts):
+        fetch(c).start()
+    sampled = rows_ref[...] & (ROWS_DEV - 1)
+    ones = jnp.ones((sampled.shape[1], B), bf16)
+    for start in range(0, ROWS_DEV, 256):
+        place = lax.broadcasted_iota(jnp.int32, (256, sampled.shape[1]), 0) + start
+        hit = jnp.where(place == sampled, 1.0, 0.0).astype(bf16)
+        out_ref[start : start + 256, COLS:] = dg(hit, ones, 1, 0).astype(bf16)
+    put(parts).start()
+    signs = sign_ref[...].astype(f32)
+    tables = [(table_ref[...] * signs[b : b + 1, :]).astype(bf16) for b in range(blocks)]
+    for c in range(parts):
+        fetch(c).wait()
+        lanes = slice(c * width, (c + 1) * width)
+        mixed = []
         for b in range(blocks):
-            signed = table_ref[...] * sign_ref[b : b + 1, :]
-            inner = dg(signed.astype(bf16), x_ref[b * FACTOR : (b + 1) * FACTOR, lane : lane + width], 1, 0)
-            parts.append(inner.astype(bf16).astype(f32))
+            inner = dg(tables[b], x_ref[b * FACTOR : (b + 1) * FACTOR, lanes], 1, 0)
+            mixed.append(inner.astype(bf16).astype(f32))
         step = 1
         while step < blocks:
-            parts = [
-                parts[b] + parts[b ^ step] if not b & step else parts[b ^ step] - parts[b]
+            mixed = [
+                mixed[b] + mixed[b ^ step] if not b & step else mixed[b ^ step] - mixed[b]
                 for b in range(blocks)
             ]
             step *= 2
         for b in range(blocks):
-            out_ref[b * FACTOR : (b + 1) * FACTOR, lane : lane + width] = parts[b].astype(bf16)
-    for start in range(0, ROWS_DEV, 256):
-        place = lax.broadcasted_iota(jnp.int32, (256, B), 0) + start
-        hit = jnp.where(place == rows_ref[...], 1.0, 0.0).astype(bf16)
-        ones = jnp.ones((B, B), bf16)
-        out_ref[start : start + 256, COLS:] = dg(hit, ones, 1, 0).astype(bf16)
-
-
-def transform(features, signs, local_rows):
-    rows = jnp.concatenate([local_rows, jnp.full((B - local_rows.shape[0],), -1, jnp.int32)])[None, :]
+            out_ref[b * FACTOR : (b + 1) * FACTOR, lanes] = mixed[b].astype(bf16)
+        put(c).start()
+    for c in range(parts + 1):
+        put(c).wait()
+
+
+def transform(features, flip_signs, sample_rows):
+    parts = COLS // 256
     return pl.pallas_call(
         transform_kernel,
         out_shape=jax.ShapeDtypeStruct((ROWS_DEV, COLS + B), bf16),
-        in_specs=[VMEM] * 4,
-        out_specs=VMEM,
-        compiler_params=pltpu.CompilerParams(vmem_limit_bytes=40 << 20),
+        in_specs=[ANY] + [VMEM] * 3,
+        out_specs=ANY,
+        scratch_shapes=[
+            pltpu.VMEM((ROWS_DEV, COLS), bf16),
+            pltpu.VMEM((ROWS_DEV, COLS + B), bf16),
+            pltpu.SemaphoreType.DMA((parts,)),
+            pltpu.SemaphoreType.DMA((parts + 1,)),
+        ],
+        compiler_params=pltpu.CompilerParams(vmem_limit_bytes=16 << 20),
         name="transform",
-    )(features, signs.astype(f32).reshape(ROWS_DEV // FACTOR, FACTOR), jnp.asarray(hadamard(FACTOR)), rows)
-
-
-def combine_kernel(core_ref, p_ref, table_ref, block_ref, mine_ref, other_ref, x_ref):
-    core = core_ref[0]
+    )(
+        features,
+        flip_signs.reshape(ROWS_DEV // FACTOR, FACTOR),
+        sample_rows.reshape(1, -1),
+        jnp.asarray(hadamard(FACTOR)),
+    )
+
+
+def combine_kernel(p_ref, table_ref, block_ref, mine_ref, other_ref, x_ref):
+    core = lax.axis_index("rows") % 2
     mask = p_ref[:, COLS:].astype(f32)
     row = lax.broadcasted_iota(jnp.int32, (ROWS_DEV, B), 0)
     lane = lax.broadcasted_iota(jnp.int32, (ROWS_DEV, B), 1)
@@ -136,7 +168,7 @@
         done += count
 
 
-def combine(core, pieces):
+def combine(pieces):
     order = np.concatenate([np.arange(0, DEVICES, 2), np.arange(1, DEVICES, 2)])
     table = np.repeat(hadamard(DEVICES)[order], GROUP, axis=1)
     block = np.repeat(np.eye(DEVICES, dtype=np.float32)[order], GROUP, axis=1)
@@ -144,12 +176,12 @@
     return pl.pallas_call(
         combine_kernel,
         out_shape=(shape, shape),
-        in_specs=[SMEM, VMEM, VMEM, VMEM],
+        in_specs=[VMEM] * 3,
         out_specs=(VMEM, VMEM),
         scratch_shapes=[pltpu.VMEM((2 * CHIPS * CHUNK, B), f32)],
-        compiler_params=pltpu.CompilerParams(vmem_limit_bytes=40 << 20),
+        compiler_params=pltpu.CompilerParams(vmem_limit_bytes=24 << 20),
         name="combine",
-    )(core, pieces, jnp.asarray(table, bf16), jnp.asarray(block, bf16))
+    )(pieces, jnp.asarray(table, bf16), jnp.asarray(block, bf16))
 
 
 def factor_rows(s_ref, i):
@@ -188,7 +220,7 @@
             s_ref[base + 8 * v : base + 8 * v + 8, h * B : (h + 1) * B] = R[v][h]
 
 
-def finish_panel(p, f_ref, u_ref, a_ref, s_ref, uh_ref, ul_ref, xh_ref, xl_ref, acc_ref):
+def finish_panel(p, load, store, f_ref, u_ref, a_ref, s_ref, uh_ref, ul_ref, xh_ref, xl_ref, acc_ref):
     o = p * B
     e = o + B
     ri = lax.broadcasted_iota(jnp.int32, (B, B), 0)
@@ -206,6 +238,7 @@
             left = jnp.concatenate([high[:, c : c + B], high[:, c : c + B], low[:, c : c + B]], axis=0)
             right = jnp.concatenate([high[:, c:], low[:, c:], high[:, c:]], axis=0)
             a_ref[q * B : (q + 1) * B, q * B :] -= dg(left, right, 0, 0)
+    store.start()
     corner = split(inverse.T)
     if p > 0:
         above = dot3s((xh_ref[:o, :o], xl_ref[:o, :o]), (uh_ref[:o, o:e], ul_ref[:o, o:e]))
@@ -214,6 +247,8 @@
     if e < COLS:
         xh_ref[e:, o:e] = jnp.zeros((COLS - e, B), bf16)
         xl_ref[e:, o:e] = jnp.zeros((COLS - e, B), bf16)
+    if p == 1:
+        load.wait()
     if p % 2:
         pair = slice(o - B, e)
         w = dg(f_ref[:, :e], xh_ref[:e, pair], 1, 0) + dg(f_ref[:, :e], xl_ref[:e, pair], 1, 0)
@@ -221,14 +256,20 @@
 
 
 def factor_kernel(
-    meta_ref, mine_ref, other_ref, rows_ref, f_ref, u_ref, lev_ref, sk_ref,
-    a_ref, s_ref, uh_ref, ul_ref, xh_ref, xl_ref, acc_ref,
+    sample_ref, mine_ref, other_ref, got_ref, f_hbm, u_hbm, lev_hbm, sk_hbm,
+    a_ref, s_ref, uh_ref, ul_ref, xh_ref, xl_ref, acc_ref, f_ref, u_ref, lev_ref, sk_ref, sem, u_sem,
 ):
-    core = meta_ref[0]
+    load = pltpu.make_async_copy(f_hbm, f_ref, sem.at[0])
+    load.start()
+    core = lax.axis_index("rows") % 2
     for k in range(SAMPLES // DEVICES):
-        q = meta_ref[1 + k] // GROUP
+        q = (sample_ref[k] & (ROWS_DEV - 1)) // GROUP
         spot = jnp.bitwise_xor(q % 2, core)
-        sk_ref[k] = rows_ref[q // 2, pl.ds(pl.multiple_of(spot * GROUP, GROUP), GROUP), :]
+        row = got_ref[q // 2, pl.ds(pl.multiple_of(SHARE + spot * GROUP, GROUP), GROUP), :]
+        for b in range(NB):
+            sk_ref[k : k + 1, b * B : (b + 1) * B] = row[b : b + 1, :]
+    rows_out = pltpu.make_async_copy(sk_ref, sk_hbm, sem.at[1])
+    rows_out.start()
     first = core == 0
     for r in range(NB):
         for c in range(r, NB):
@@ -241,6 +282,10 @@
     ri = lax.broadcasted_iota(jnp.int32, (B, B), 0)
     ci = lax.broadcasted_iota(jnp.int32, (B, B), 1)
 
+    def store(p):
+        rows = pl.ds(p * B, B)
+        return pltpu.make_async_copy(u_ref.at[rows, :], u_hbm.at[rows, :], u_sem.at[p])
+
     def panel(p, _):
         o = pl.multiple_of(p * B, B)
         s_ref[:, :B] = a_ref[pl.ds(o, B), pl.ds(o, B)]
@@ -255,43 +300,55 @@
 
             @pl.when(p == static)
             def _():
-                finish_panel(static, f_ref, u_ref, a_ref, s_ref, uh_ref, ul_ref, xh_ref, xl_ref, acc_ref)
+                finish_panel(static, load, store(static), f_ref, u_ref, a_ref, s_ref, uh_ref, ul_ref, xh_ref, xl_ref, acc_ref)
 
         return 0
 
     lax.fori_loop(0, NB, panel, 0)
     high, low = split(acc_ref[...])
     weight = jnp.full((8, 2 * B), float(DEVICES * ROWS_DEV // COLS), bf16)
-    lev_ref[...] = dg(weight, high, 1, 1) + dg(weight, low, 1, 1)
-
-
-def factor(meta, mine, other, rows, features):
+    lev_ref[...] = (dg(weight, high, 1, 1) + dg(weight, low, 1, 1))[:1, :]
+    lev_out = pltpu.make_async_copy(lev_ref, lev_hbm, sem.at[2])
+    lev_out.start()
+    rows_out.wait()
+    for p in range(NB):
+        store(p).wait()
+    lev_out.wait()
+
+
+def factor(sample_rows, mine, other, got, features):
+    samples = SAMPLES // DEVICES
     return pl.pallas_call(
         factor_kernel,
         out_shape=(
             jax.ShapeDtypeStruct((COLS, COLS), f32),
-            jax.ShapeDtypeStruct((8, ROWS_DEV), f32),
-            jax.ShapeDtypeStruct((SAMPLES // DEVICES, GROUP, B), f32),
+            jax.ShapeDtypeStruct((1, ROWS_DEV), f32),
+            jax.ShapeDtypeStruct((samples, COLS), f32),
         ),
-        in_specs=[SMEM] + [VMEM] * 4,
-        out_specs=(VMEM,) * 3,
+        in_specs=[SMEM, VMEM, VMEM, VMEM, ANY],
+        out_specs=(ANY,) * 3,
         scratch_shapes=[pltpu.VMEM((COLS, COLS), f32), pltpu.VMEM((B, 2 * B), f32)]
         + [pltpu.VMEM((COLS, COLS), bf16)] * 4
-        + [pltpu.VMEM((ROWS_DEV, 2 * B), f32)],
-        compiler_params=pltpu.CompilerParams(vmem_limit_bytes=60 << 20),
+        + [
+            pltpu.VMEM((ROWS_DEV, 2 * B), f32),
+            pltpu.VMEM((ROWS_DEV, COLS), bf16),
+            pltpu.VMEM((COLS, COLS), f32),
+            pltpu.VMEM((1, ROWS_DEV), f32),
+            pltpu.VMEM((samples, COLS), f32),
+            pltpu.SemaphoreType.DMA((3,)),
+            pltpu.SemaphoreType.DMA((NB,)),
+        ],
+        compiler_params=pltpu.CompilerParams(vmem_limit_bytes=32 << 20),
         name="factor",
-    )(meta, mine, other, rows, features)
+    )(sample_rows, mine, other, got, features)
 
 
 def shards(features, flip_signs, sample_rows):
-    position = lax.axis_index("rows")
-    core = position % 2
-    local_rows = sample_rows - position * ROWS_DEV
-    mixed = transform(features, flip_signs, local_rows)
+    mixed = transform(features, flip_signs, sample_rows)
     pieces = lax.all_to_all(
         mixed.reshape(DEVICES, GROUP, COLS + B), "rows", split_axis=0, concat_axis=0, tiled=True
     ).reshape(ROWS_DEV, COLS + B)
-    mine, other = combine(core[None], pieces)
+    mine, other = combine(pieces)
     swap = [(d, d ^ 1) for d in range(DEVICES)]
     came = lax.ppermute(other, "rows", swap).reshape(CHIPS, CHUNK, B)
     mine = mine.reshape(CHIPS, CHUNK, B)
@@ -306,9 +363,8 @@
         "rows", split_axis=0, concat_axis=0, tiled=True, axis_index_groups=same_core,
     ).reshape(HALF_TILES * B, B)
     far = lax.ppermute(half, "rows", swap)
-    meta = jnp.concatenate([core[None], local_rows])
-    upper, lev, sketch = factor(meta, half, far, got[:, SHARE:], features)
-    return sketch.reshape(-1, COLS), upper, lev[0]
+    upper, lev, sketch = factor(sample_rows, half, far, got, features)
+    return sketch, upper, lev.reshape(-1)
 
 
 def solution(mesh):

time: 175 us -> 168 us (0.960)
  blocking collectives: 54.6 us -> 98.9 us
  waiting for transfers between devices: 37.2 us -> 5.68 us
  starting transfers between devices: 16.3 us -> 4.83 us
  local copies, waits for them, and re-layouts: 8.82 us -> 3.92 us
  other arithmetic: 2.33 us -> 0.4 us
    all_to_all x0 -> x1, blocking collectives: none -> 44.2 us  [shards(): lax.all_to_all(mixed.reshape(DEVICES, GROUP, COLS + B), 'rows', split_axi...]
    all_to_all x1 -> x0, waiting for transfers between devices: 32.9 us -> none  [shards(): lax.all_to_all(mixed.reshape(DEVICES, GROUP, COLS + B), 'rows', split_axi...]
    all_to_all x1 -> x0, starting transfers between devices: 11.5 us -> none  [shards(): lax.all_to_all(mixed.reshape(DEVICES, GROUP, COLS + B), 'rows', split_axi...]
    pallas_call x1, Pallas kernels: 51.6 us -> 48.7 us  [factor(): pl.pallas_call(factor_kernel, out_shape=(jax.ShapeDtypeStruct((COLS, COLS...]
    unnamed x15 -> x16, local copies, waits for them, and re-layouts: 6.49 us -> 3.79 us
    slice x2 -> x0, local copies, waits for them, and re-layouts: 2.19 us -> none  [the longest x1 1.35 us: shards(): return (sketch.reshape(-1, COLS), upper, lev[0])]
  transfers between devices with their start and end apart: 3 -> 2, of which waited for: 3 -> 2; matrix products, arithmetic and copies ran while one was open for 1% -> 0% of each run, Pallas kernels for 0% -> 0%
where the time goes in v3:
time: 168 us
  blocking collectives  98.9 us (59%)
  Pallas kernels  53.2 us (32%)
  waiting for transfers between devices  5.68 us (3%)
  starting transfers between devices  4.83 us (3%)
  local copies, waits for them, and re-layouts  3.92 us (2%)
    pallas_call x1, Pallas kernels, factor(): pl.pallas_call(factor_kernel, out_shape=(jax.ShapeDtypeStruct((COLS, COLS...  48.7 us
    all_to_all x1, blocking collectives, shards(): lax.all_to_all(mixed.reshape(DEVICES, GROUP, COLS + B), 'rows', split_axi...  44.2 us
    all_to_all x1, blocking collectives, shards(): lax.all_to_all(shares, 'rows', split_axis=0, concat_axis=0, tiled=True, a...  29.8 us
    all_to_all x1, blocking collectives, shards(): lax.all_to_all(jnp.broadcast_to(total[None], (CHIPS, SHARE, B)), 'rows',...  24.9 us
    unnamed x16, local copies, waits for them, and re-layouts  3.79 us
    ppermute x1, starting transfers between devices, shards(): far = lax.ppermute(half, 'rows', swap)  3.48 us
  transfers between devices with their start and end apart: 2, of which 2 were waited for; matrix products, arithmetic and copies ran while one was open for 0% of the time, Pallas kernels for 0%

profile of v3, /device:TPU:1, one launch (start us, length us, event | category | flops | bytes accessed | tf_op | source)
XLA Modules:
  0.0 167.8 jit_solution(12206074353842266914)
XLA Ops:
  0.6 0.0 copy-start
  0.6 1.6 copy-done
  2.2 0.0 copy-start.4
  2.2 0.8 copy-done.4
  3.1 0.0 copy-start.5
  3.1 0.7 copy-done.5
  3.8 0.0 copy-start.6
  3.8 0.7 copy-done.6
  4.4 2.3 %transform.1 = bf16[1024,1152]{1,0:T(8,128)(2,1)S(1)} custom-call(bf16[1024,1024]{1,0:T(8,128)(2,1)S(1)} %copy-done, s32[8,128]{1,0:T(8,128)S(1)} %bitcast.14, s32[1,32]{1,0:T(1,128)S(1)} %bitcast.15, f32[128,128]{1,0:T(8,128)S(1)} %copy-done.4), custom_call_target="tpu_custom_call" | custom-call | tf_op jit(solution)/shard_map/transform/pallas_call | solution.py:109
  6.7 0.0 copy-start.2
  6.7 0.0 copy-start.3
  6.7 44.2 %all_to_all.15 = bf16[128,8,1152]{2,1,0:T(8,128)(2,1)S(1)} all-to-all(bf16[128,8,1152]{2,1,0:T(8,128)(2,1)S(1)} %bitcast.9), channel_id=1, replica_groups=mesh['rows'=128] {'rows'}, dimensions={0} | all-to-all | bytes 4718592 | tf_op jit(solution)/shard_map/all_to_all | solution.py:348
  50.9 0.0 copy-done.2
  51.0 0.0 copy-done.3
  51.0 2.2 %combine.1 = (f32[3072,128]{1,0:T(8,128)S(1)}, f32[3072,128]{1,0:T(8,128)S(1)}) custom-call(bf16[1024,1152]{1,0:T(8,128)(2,1)S(1)} %bitcast.8, bf16[128,1024]{1,0:T(8,128)(2,1)S(1)} %copy-done.3, bf16[128,1024]{1,0:T(8,128)(2,1)S(1)} %copy-done.2), custom_call_target="tpu_custom_call" | custom-call | tf_op jit(solution)/shard_map/combine/pallas_call | solution.py:176
  53.2 1.4 collective-permute-start
  54.6 3.0 %collective-permute-done = f32[3072,128]{1,0:T(8,128)S(1)} collective-permute-done((f32[3072,128]{1,0:T(8,128)S(1)}, f32[3072,128]{1,0:T(8,128)S(1)}, u32[]{:S(2)}, u32[]{:S(2)}) %collective-permute-start) | collective-permute-done | bytes 1572896 | tf_op jit(solution)/shard_map/ppermute | solution.py:353
  57.6 0.2 slice_add_fusion
  57.8 0.1 pad_maximum_fusion
  57.9 29.8 %all_to_all.16.got_ref = f32[64,56,128]{2,1,0:T(8,128)S(1)} all-to-all(f32[64,56,128]{2,1,0:T(8,128)S(1)} %pad_maximum_fusion), channel_id=1, replica_groups={{0,2,4,6,8,10,12,14,16,18,20,22,24,26,28,30,32,34,36,38,40,42,44,46,48,..., dimensions={0} | all-to-all | bytes 3670016 | tf_op jit(solution)/shard_map/all_to_all | solution.py:357
  87.7 0.1 slice_reduce_fusion
  87.8 0.1 broadcast_in_dim.2
  87.9 0.0 copy-start.1
  87.9 0.0 copy-start.7
  88.0 24.9 %all_to_all.17 = f32[64,40,128]{2,1,0:T(8,128)S(1)} all-to-all(f32[64,40,128]{2,1,0:T(8,128)S(1)} %broadcast_in_dim.2), channel_id=1, replica_groups={{0,2,4,6,8,10,12,14,16,18,20,22,24,26,28,30,32,34,36,38,40,42,44,46,48,..., dimensions={0} | all-to-all | bytes 2621440 | tf_op jit(solution)/shard_map/all_to_all | solution.py:361
  112.8 3.5 %collective-permute-start.1 = (f32[2560,128]{1,0:T(8,128)S(1)}, f32[2560,128]{1,0:T(8,128)S(1)}, u32[]{:S(2)}, u32[]{:S(2)}) collective-permute-start(f32[2560,128]{1,0:T(8,128)S(1)} %bitcast.10), channel_id=1, source_target_pairs={{0,1},{1,0},{2,3},{3,2},{4,5},{5,4},{6,7},{7,6},{8,9},{9,8},{10,11... | collective-permute-start | bytes 3932168 | tf_op jit(solution)/shard_map/ppermute | solution.py:365
  116.3 2.7 %collective-permute-done.1.other_ref = f32[2560,128]{1,0:T(8,128)S(1)} collective-permute-done((f32[2560,128]{1,0:T(8,128)S(1)}, f32[2560,128]{1,0:T(8,128)S(1)}, u32[]{:S(2)}, u32[]{:S(2)}) %collective-permute-start.1) | collective-permute-done | bytes 1310752 | tf_op jit(solution)/shard_map/ppermute | solution.py:365
  119.0 0.0 copy-done.1
  119.0 0.0 copy-done.7
  119.0 48.7 %factor.1 = (f32[1024,1024]{1,0:T(8,128)}, f32[1,1024]{1,0:T(1,128)}, f32[32,1024]{1,0:T(8,128)}) custom-call(s32[32]{0:T(128)S(1)} %copy-done.7, f32[2560,128]{1,0:T(8,128)S(1)} %bitcast.11, f32[2560,128]{1,0:T(8,128)S(1)} %collective-permute-done.1.other_ref, f32[64,56,128]{2,1,0:T(8,128)S(1)} %all_to_all.16.got_ref, bf16[1024,1024]{1,0:T(8,128)(2,1)S(1)} %copy-done.1), custom_call_target="tpu_custom_call" | custom-call | tf_op jit(solution)/shard_map/factor/pallas_call | solution.py:321
  (2 shorter events, 0.0 us)
Async XLA Ops:
  0.6 1.6 copy-start
  2.2 0.8 copy-start.4
  3.1 0.7 copy-start.5
  3.8 0.7 copy-start.6
  6.7 44.2 %copy-start.2 = (bf16[128,1024]{1,0:T(8,128)(2,1)S(1)}, bf16[128,1024]{1,0:T(8,128)(2,1)}, u32[]{:S(2)}) copy-start(bf16[128,1024]{1,0:T(8,128)(2,1)} %constant.10.clone.block_ref) | copy-start | bytes 786436
  6.7 44.2 %copy-start.3 = (bf16[128,1024]{1,0:T(8,128)(2,1)S(1)}, bf16[128,1024]{1,0:T(8,128)(2,1)}, u32[]{:S(2)}) copy-start(bf16[128,1024]{1,0:T(8,128)(2,1)} %constant.9.clone.table_ref) | copy-start | bytes 786436
  53.2 4.4 %collective-permute-start = (f32[3072,128]{1,0:T(8,128)S(1)}, f32[3072,128]{1,0:T(8,128)S(1)}, u32[]{:S(2)}, u32[]{:S(2)}) collective-permute-start(f32[3072,128]{1,0:T(8,128)S(1)} %get-tuple-element.9), channel_id=1, source_target_pairs={{0,1},{1,0},{2,3},{3,2},{4,5},{5,4},{6,7},{7,6},{8,9},{9,8},{10,11... | collective-permute-start | bytes 4718600 | tf_op jit(solution)/shard_map/ppermute | solution.py:353
  87.9 31.0 %copy-start.1 = (bf16[1024,1024]{1,0:T(8,128)(2,1)S(1)}, bf16[1024,1024]{1,0:T(8,128)(2,1)}, u32[]{:S(2)}) copy-start(bf16[1024,1024]{1,0:T(8,128)(2,1)} %f_hbm.1) | copy-start | bytes 6291460
  87.9 31.0 %copy-start.7 = (s32[32]{0:T(128)S(1)}, s32[32]{0:T(128)}, u32[]{:S(2)}) copy-start(s32[32]{0:T(128)} %sample_ref.1) | copy-start | bytes 388
  112.8 6.1 %collective-permute-start.1 = (f32[2560,128]{1,0:T(8,128)S(1)}, f32[2560,128]{1,0:T(8,128)S(1)}, u32[]{:S(2)}, u32[]{:S(2)}) collective-permute-start(f32[2560,128]{1,0:T(8,128)S(1)} %bitcast.10), channel_id=1, source_target_pairs={{0,1},{1,0},{2,3},{3,2},{4,5},{5,4},{6,7},{7,6},{8,9},{9,8},{10,11... | collective-permute-start | bytes 3932168 | tf_op jit(solution)/shard_map/ppermute | solution.py:365

commit v4 on v3

--- a/solution.py
+++ b/solution.py
@@ -2,7 +2,6 @@
 
 import jax
 import jax.numpy as jnp
-import numpy as np
 from jax import lax
 from jax.experimental import pallas as pl
 from jax.experimental.pallas import tpu as pltpu
@@ -17,13 +16,14 @@
 CHIPS = 64
 B = 128
 NB = COLS // B
-SB = 32
+SB = 64
 HALF_TILES = 20
 SHARE = HALF_TILES * B // CHIPS
 CHUNK = SHARE + GROUP
 f32 = jnp.float32
 bf16 = jnp.bfloat16
 ANY = pl.BlockSpec(memory_space=pl.ANY)
+HBM = pl.BlockSpec(memory_space=pltpu.HBM)
 VMEM = pl.BlockSpec(memory_space=pltpu.VMEM)
 SMEM = pl.BlockSpec(memory_space=pltpu.SMEM)
 
@@ -41,25 +41,23 @@
     return high, (x - high.astype(f32)).astype(bf16)
 
 
-def dot3s(a, b, ca=1, cb=0):
+def dot3(a, b, ca=1, cb=0):
     (ah, al), (bh, bl) = a, b
     return dg(ah, bh, ca, cb) + dg(ah, bl, ca, cb) + dg(al, bh, ca, cb)
 
 
-def dot3(a, b, ca=1, cb=0):
-    return dot3s(split(a), split(b), ca, cb)
-
-
-def hadamard(dimension):
-    positions = np.arange(dimension)
-    common = positions[:, None] & positions[None, :]
-    parity = np.zeros((dimension, dimension), np.int32)
-    for bit in range(dimension.bit_length() - 1):
-        parity ^= common >> bit & 1
-    return (1 - 2 * parity).astype(np.float32)
-
-
-def transform_kernel(x_hbm, sign_ref, rows_ref, table_ref, out_hbm, x_ref, out_ref, in_sem, out_sem):
+def iota(shape, dim):
+    return lax.broadcasted_iota(jnp.int32, shape, dim)
+
+
+def hadamard(rows, cols):
+    bits = rows & cols
+    for shift in (4, 2, 1):
+        bits = bits ^ (bits >> shift)
+    return (1 - 2 * (bits & 1)).astype(f32)
+
+
+def transform_kernel(x_hbm, sign_hbm, rows_hbm, out_hbm, x_ref, out_ref, sign_ref, rows_ref, in_sem, out_sem, sem):
     blocks = ROWS_DEV // FACTOR
     width = 256
     parts = COLS // width
@@ -72,8 +70,15 @@
         lanes = pl.ds(c * width, width) if c < parts else pl.ds(COLS, B)
         return pltpu.make_async_copy(out_ref.at[:, lanes], out_hbm.at[:, lanes], out_sem.at[c])
 
+    sign_in = pltpu.make_async_copy(sign_hbm, sign_ref, sem.at[0])
+    rows_in = pltpu.make_async_copy(rows_hbm, rows_ref, sem.at[1])
+    rows_in.start()
+    sign_in.start()
     for c in range(parts):
         fetch(c).start()
+    square = (FACTOR, FACTOR)
+    table = hadamard(iota(square, 0), iota(square, 1))
+    rows_in.wait()
     sampled = rows_ref[...] & (ROWS_DEV - 1)
     ones = jnp.ones((sampled.shape[1], B), bf16)
     for start in range(0, ROWS_DEV, 256):
@@ -81,8 +86,9 @@
         hit = jnp.where(place == sampled, 1.0, 0.0).astype(bf16)
         out_ref[start : start + 256, COLS:] = dg(hit, ones, 1, 0).astype(bf16)
     put(parts).start()
+    sign_in.wait()
     signs = sign_ref[...].astype(f32)
-    tables = [(table_ref[...] * signs[b : b + 1, :]).astype(bf16) for b in range(blocks)]
+    tables = [(table * signs[b : b + 1, :]).astype(bf16) for b in range(blocks)]
     for c in range(parts):
         fetch(c).wait()
         lanes = slice(c * width, (c + 1) * width)
@@ -109,13 +115,16 @@
     return pl.pallas_call(
         transform_kernel,
         out_shape=jax.ShapeDtypeStruct((ROWS_DEV, COLS + B), bf16),
-        in_specs=[ANY] + [VMEM] * 3,
+        in_specs=[HBM] * 3,
         out_specs=ANY,
         scratch_shapes=[
             pltpu.VMEM((ROWS_DEV, COLS), bf16),
             pltpu.VMEM((ROWS_DEV, COLS + B), bf16),
+            pltpu.VMEM((ROWS_DEV // FACTOR, FACTOR), jnp.int32),
+            pltpu.VMEM((1, SAMPLES // DEVICES), jnp.int32),
             pltpu.SemaphoreType.DMA((parts,)),
             pltpu.SemaphoreType.DMA((parts + 1,)),
+            pltpu.SemaphoreType.DMA((2,)),
         ],
         compiler_params=pltpu.CompilerParams(vmem_limit_bytes=16 << 20),
         name="transform",
@@ -123,18 +132,22 @@
         features,
         flip_signs.reshape(ROWS_DEV // FACTOR, FACTOR),
         sample_rows.reshape(1, -1),
-        jnp.asarray(hadamard(FACTOR)),
     )
 
 
-def combine_kernel(p_ref, table_ref, block_ref, mine_ref, other_ref, x_ref):
+def combine_kernel(p_ref, mine_ref, other_ref, x_ref):
     core = lax.axis_index("rows") % 2
     mask = p_ref[:, COLS:].astype(f32)
     row = lax.broadcasted_iota(jnp.int32, (ROWS_DEV, B), 0)
     lane = lax.broadcasted_iota(jnp.int32, (ROWS_DEV, B), 1)
     mask = jnp.where((row & (GROUP - 1)) == (lane & (GROUP - 1)), mask, 0.0).astype(bf16)
-    pick = dg(block_ref[...], mask, 1, 0).astype(bf16)
-    mixer = table_ref[...] * jnp.concatenate([pick] * GROUP, axis=1)
+    shape = (DEVICES, DEVICES * GROUP)
+    place = iota(shape, 0)
+    target = 2 * (place & (CHIPS - 1)) + place // CHIPS
+    source = iota(shape, 1) // GROUP
+    block = jnp.where(target == source, 1.0, 0.0).astype(bf16)
+    pick = dg(block, mask, 1, 0)
+    mixer = (hadamard(target, source) * jnp.concatenate([pick] * GROUP, axis=1)).astype(bf16)
     rows = dg(mixer, p_ref[:, :COLS], 1, 0) * (1.0 / math.sqrt(SAMPLES))
     for b in range(NB):
         for half in range(2):
@@ -169,19 +182,16 @@
 
 
 def combine(pieces):
-    order = np.concatenate([np.arange(0, DEVICES, 2), np.arange(1, DEVICES, 2)])
-    table = np.repeat(hadamard(DEVICES)[order], GROUP, axis=1)
-    block = np.repeat(np.eye(DEVICES, dtype=np.float32)[order], GROUP, axis=1)
     shape = jax.ShapeDtypeStruct((CHIPS * CHUNK, B), f32)
     return pl.pallas_call(
         combine_kernel,
         out_shape=(shape, shape),
-        in_specs=[VMEM] * 3,
+        in_specs=[VMEM],
         out_specs=(VMEM, VMEM),
         scratch_shapes=[pltpu.VMEM((2 * CHIPS * CHUNK, B), f32)],
         compiler_params=pltpu.CompilerParams(vmem_limit_bytes=24 << 20),
         name="combine",
-    )(pieces, jnp.asarray(table, bf16), jnp.asarray(block, bf16))
+    )(pieces)
 
 
 def factor_rows(s_ref, i):
@@ -196,7 +206,7 @@
     for g in range(groups):
         lane = base + 8 * g
         rest = range(groups - g)
-        C = [[jnp.broadcast_to(R[g + v][0][:, lane + k : lane + k + 1], (8, B)) for v in rest] for k in range(8)]
+        C = [[jnp.take_along_axis(R[g + v][0], jnp.full((8, B), lane + k, jnp.int32), axis=1) for v in rest] for k in range(8)]
         scale = None
         for k in range(8):
             pivot = spread(C[k][0], k)
@@ -228,7 +238,7 @@
     inverse = jnp.where(ri >= ci, s_ref[:, B:], 0.0)
     u_ref[o:e, o:e] = jnp.where(ri <= ci, s_ref[:, :B], 0.0)
     if e < COLS:
-        across = dot3s(split(inverse), split(a_ref[o:e, e:]))
+        across = dot3(split(inverse), split(a_ref[o:e, e:]))
         u_ref[o:e, e:] = across
         high, low = split(across)
         uh_ref[o:e, e:] = high
@@ -241,8 +251,8 @@
     store.start()
     corner = split(inverse.T)
     if p > 0:
-        above = dot3s((xh_ref[:o, :o], xl_ref[:o, :o]), (uh_ref[:o, o:e], ul_ref[:o, o:e]))
-        xh_ref[:o, o:e], xl_ref[:o, o:e] = split(-dot3s(split(above), corner))
+        above = dot3((xh_ref[:o, :o], xl_ref[:o, :o]), (uh_ref[:o, o:e], ul_ref[:o, o:e]))
+        xh_ref[:o, o:e], xl_ref[:o, o:e] = split(-dot3(split(above), corner))
     xh_ref[o:e, o:e], xl_ref[o:e, o:e] = corner
     if e < COLS:
         xh_ref[e:, o:e] = jnp.zeros((COLS - e, B), bf16)
@@ -257,7 +267,7 @@
 
 def factor_kernel(
     sample_ref, mine_ref, other_ref, got_ref, f_hbm, u_hbm, lev_hbm, sk_hbm,
-    a_ref, s_ref, uh_ref, ul_ref, xh_ref, xl_ref, acc_ref, f_ref, u_ref, lev_ref, sk_ref, sem, u_sem,
+    a_ref, panels_ref, uh_ref, ul_ref, xh_ref, xl_ref, acc_ref, f_ref, u_ref, lev_ref, sk_ref, sem, u_sem,
 ):
     load = pltpu.make_async_copy(f_hbm, f_ref, sem.at[0])
     load.start()
@@ -286,25 +296,20 @@
         rows = pl.ds(p * B, B)
         return pltpu.make_async_copy(u_ref.at[rows, :], u_hbm.at[rows, :], u_sem.at[p])
 
-    def panel(p, _):
-        o = pl.multiple_of(p * B, B)
-        s_ref[:, :B] = a_ref[pl.ds(o, B), pl.ds(o, B)]
+    for p in range(NB):
+        o = p * B
+        s_ref = panels_ref.at[p % 2]
+        s_ref[:, :B] = a_ref[o : o + B, o : o + B]
         s_ref[:, B:] = jnp.where(ri == ci, 1.0, 0.0).astype(f32)
         for i in range(B // SB):
             factor_rows(s_ref, i)
-            if i < B // SB - 1:
-                R = s_ref[i * SB : (i + 1) * SB, :]
-                update = dot3(R[:, :B], R, 0, 0)
-                s_ref[(i + 1) * SB :, :] = s_ref[(i + 1) * SB :, :] - update[(i + 1) * SB :, :]
-        for static in range(NB):
-
-            @pl.when(p == static)
-            def _():
-                finish_panel(static, load, store(static), f_ref, u_ref, a_ref, s_ref, uh_ref, ul_ref, xh_ref, xl_ref, acc_ref)
-
-        return 0
-
-    lax.fori_loop(0, NB, panel, 0)
+            done = (i + 1) * SB
+            if done < B:
+                high, low = split(s_ref[i * SB : done, :])
+                left = jnp.concatenate([high[:, :B], high[:, :B], low[:, :B]], axis=0)
+                right = jnp.concatenate([high, low, high], axis=0)
+                s_ref[done:, :] = s_ref[done:, :] - dg(left, right, 0, 0)[done:]
+        finish_panel(p, load, store(p), f_ref, u_ref, a_ref, s_ref, uh_ref, ul_ref, xh_ref, xl_ref, acc_ref)
     high, low = split(acc_ref[...])
     weight = jnp.full((8, 2 * B), float(DEVICES * ROWS_DEV // COLS), bf16)
     lev_ref[...] = (dg(weight, high, 1, 1) + dg(weight, low, 1, 1))[:1, :]
@@ -327,7 +332,7 @@
         ),
         in_specs=[SMEM, VMEM, VMEM, VMEM, ANY],
         out_specs=(ANY,) * 3,
-        scratch_shapes=[pltpu.VMEM((COLS, COLS), f32), pltpu.VMEM((B, 2 * B), f32)]
+        scratch_shapes=[pltpu.VMEM((COLS, COLS), f32), pltpu.VMEM((2, B, 2 * B), f32)]
         + [pltpu.VMEM((COLS, COLS), bf16)] * 4
         + [
             pltpu.VMEM((ROWS_DEV, 2 * B), f32),

time: 168 us -> 156 us (0.929)
  Pallas kernels: 53.2 us -> 41.6 us
    pallas_call x1, Pallas kernels: 48.7 us -> 37 us  [factor(): pl.pallas_call(factor_kernel, out_shape=(jax.ShapeDtypeStruct((COLS, COLS...]
    unnamed x16 -> x10, local copies, waits for them, and re-layouts: 3.79 us -> 2.94 us
where the time goes in v4:
time: 156 us; the launch traced here: 155 us
  blocking collectives  98.9 us (63%)
  Pallas kernels  41.6 us (27%)
  waiting for transfers between devices  5.68 us (4%)
  starting transfers between devices  4.83 us (3%)
  local copies, waits for them, and re-layouts  3.07 us (2%)
    all_to_all x1, blocking collectives, shards(): lax.all_to_all(mixed.reshape(DEVICES, GROUP, COLS + B), 'rows', split_axi...  44.2 us
    pallas_call x1, Pallas kernels, factor(): pl.pallas_call(factor_kernel, out_shape=(jax.ShapeDtypeStruct((COLS, COLS...  37 us
    all_to_all x1, blocking collectives, shards(): lax.all_to_all(shares, 'rows', split_axis=0, concat_axis=0, tiled=True, a...  29.8 us
    all_to_all x1, blocking collectives, shards(): lax.all_to_all(jnp.broadcast_to(total[None], (CHIPS, SHARE, B)), 'rows',...  24.9 us
    ppermute x1, starting transfers between devices, shards(): far = lax.ppermute(half, 'rows', swap)  3.48 us
  transfers between devices with their start and end apart: 2, of which 2 were waited for; matrix products, arithmetic and copies ran while one was open for 0% of the time, Pallas kernels for 0%

profile of v4, /device:TPU:1, one launch (start us, length us, event | category | flops | bytes accessed | tf_op | source)
XLA Modules:
  0.0 155.4 jit_solution(10824538757251561676)
XLA Ops:
  0.6 0.0 copy-start
  0.6 1.6 %copy-done = bf16[1024,1024]{1,0:T(8,128)(2,1)S(1)} copy-done((bf16[1024,1024]{1,0:T(8,128)(2,1)S(1)}, bf16[1024,1024]{1,0:T(8,128)(2,1)}, u32[]{:S(2)}) %copy-start) | copy-done | bytes 2097176
  2.2 0.0 copy-start.2
  2.2 0.7 copy-done.2
  2.9 0.0 copy-start.3
  2.9 0.7 copy-done.3
  3.6 2.4 %transform.1 = bf16[1024,1152]{1,0:T(8,128)(2,1)S(1)} custom-call(bf16[1024,1024]{1,0:T(8,128)(2,1)S(1)} %copy-done, s32[8,128]{1,0:T(8,128)S(1)} %bitcast.14, s32[1,32]{1,0:T(1,128)S(1)} %bitcast.15), custom_call_target="tpu_custom_call" | custom-call | tf_op jit(solution)/shard_map/transform/pallas_call | solution.py:115
  5.9 44.2 %all_to_all.15 = bf16[128,8,1152]{2,1,0:T(8,128)(2,1)S(1)} all-to-all(bf16[128,8,1152]{2,1,0:T(8,128)(2,1)S(1)} %bitcast.9), channel_id=1, replica_groups=mesh['rows'=128] {'rows'}, dimensions={0} | all-to-all | bytes 4718592 | tf_op jit(solution)/shard_map/all_to_all | solution.py:353
  50.2 2.3 %combine.1 = (f32[3072,128]{1,0:T(8,128)S(1)}, f32[3072,128]{1,0:T(8,128)S(1)}) custom-call(bf16[1024,1152]{1,0:T(8,128)(2,1)S(1)} %bitcast.8), custom_call_target="tpu_custom_call" | custom-call | tf_op jit(solution)/shard_map/combine/pallas_call | solution.py:186
  52.4 1.4 collective-permute-start
  53.8 3.0 %collective-permute-done = f32[3072,128]{1,0:T(8,128)S(1)} collective-permute-done((f32[3072,128]{1,0:T(8,128)S(1)}, f32[3072,128]{1,0:T(8,128)S(1)}, u32[]{:S(2)}, u32[]{:S(2)}) %collective-permute-start) | collective-permute-done | bytes 1572896 | tf_op jit(solution)/shard_map/ppermute | solution.py:358
  56.8 0.2 slice_add_fusion
  57.0 0.1 pad_maximum_fusion
  57.1 29.8 %all_to_all.16.got_ref = f32[64,56,128]{2,1,0:T(8,128)S(1)} all-to-all(f32[64,56,128]{2,1,0:T(8,128)S(1)} %pad_maximum_fusion), channel_id=1, replica_groups={{0,2,4,6,8,10,12,14,16,18,20,22,24,26,28,30,32,34,36,38,40,42,44,46,48,..., dimensions={0} | all-to-all | bytes 3670016 | tf_op jit(solution)/shard_map/all_to_all | solution.py:362
  86.9 0.1 slice_reduce_fusion
  87.1 0.1 broadcast_in_dim.2
  87.1 0.0 copy-start.1
  87.2 0.0 copy-start.4
  87.2 24.9 %all_to_all.17 = f32[64,40,128]{2,1,0:T(8,128)S(1)} all-to-all(f32[64,40,128]{2,1,0:T(8,128)S(1)} %broadcast_in_dim.2), channel_id=1, replica_groups={{0,2,4,6,8,10,12,14,16,18,20,22,24,26,28,30,32,34,36,38,40,42,44,46,48,..., dimensions={0} | all-to-all | bytes 2621440 | tf_op jit(solution)/shard_map/all_to_all | solution.py:366
  112.1 3.5 %collective-permute-start.1 = (f32[2560,128]{1,0:T(8,128)S(1)}, f32[2560,128]{1,0:T(8,128)S(1)}, u32[]{:S(2)}, u32[]{:S(2)}) collective-permute-start(f32[2560,128]{1,0:T(8,128)S(1)} %bitcast.10), channel_id=1, source_target_pairs={{0,1},{1,0},{2,3},{3,2},{4,5},{5,4},{6,7},{7,6},{8,9},{9,8},{10,11... | collective-permute-start | bytes 3932168 | tf_op jit(solution)/shard_map/ppermute | solution.py:370
  115.5 2.7 %collective-permute-done.1.other_ref = f32[2560,128]{1,0:T(8,128)S(1)} collective-permute-done((f32[2560,128]{1,0:T(8,128)S(1)}, f32[2560,128]{1,0:T(8,128)S(1)}, u32[]{:S(2)}, u32[]{:S(2)}) %collective-permute-start.1) | collective-permute-done | bytes 1310752 | tf_op jit(solution)/shard_map/ppermute | solution.py:370
  118.2 0.0 copy-done.1
  118.2 0.0 copy-done.4
  118.2 37.0 %factor.1 = (f32[1024,1024]{1,0:T(8,128)}, f32[1,1024]{1,0:T(1,128)}, f32[32,1024]{1,0:T(8,128)}) custom-call(s32[32]{0:T(128)S(1)} %copy-done.4, f32[2560,128]{1,0:T(8,128)S(1)} %bitcast.11, f32[2560,128]{1,0:T(8,128)S(1)} %collective-permute-done.1.other_ref, f32[64,56,128]{2,1,0:T(8,128)S(1)} %all_to_all.16.got_ref, bf16[1024,1024]{1,0:T(8,128)(2,1)S(1)} %copy-done.1), custom_call_target="tpu_custom_call" | custom-call | tf_op jit(solution)/shard_map/factor/pallas_call | solution.py:326
  (2 shorter events, 0.0 us)
Async XLA Ops:
  0.6 1.6 %copy-start = (bf16[1024,1024]{1,0:T(8,128)(2,1)S(1)}, bf16[1024,1024]{1,0:T(8,128)(2,1)}, u32[]{:S(2)}) copy-start(bf16[1024,1024]{1,0:T(8,128)(2,1)} %f_hbm.1) | copy-start | bytes 6291460
  2.2 0.7 copy-start.2
  2.9 0.7 copy-start.3
  52.4 4.4 %collective-permute-start = (f32[3072,128]{1,0:T(8,128)S(1)}, f32[3072,128]{1,0:T(8,128)S(1)}, u32[]{:S(2)}, u32[]{:S(2)}) collective-permute-start(f32[3072,128]{1,0:T(8,128)S(1)} %get-tuple-element.9), channel_id=1, source_target_pairs={{0,1},{1,0},{2,3},{3,2},{4,5},{5,4},{6,7},{7,6},{8,9},{9,8},{10,11... | collective-permute-start | bytes 4718600 | tf_op jit(solution)/shard_map/ppermute | solution.py:358
  87.1 31.1 %copy-start.1 = (bf16[1024,1024]{1,0:T(8,128)(2,1)S(1)}, bf16[1024,1024]{1,0:T(8,128)(2,1)}, u32[]{:S(2)}) copy-start(bf16[1024,1024]{1,0:T(8,128)(2,1)} %f_hbm.1) | copy-start | bytes 6291460
  87.2 31.1 %copy-start.4 = (s32[32]{0:T(128)S(1)}, s32[32]{0:T(128)}, u32[]{:S(2)}) copy-start(s32[32]{0:T(128)} %sample_ref.1) | copy-start | bytes 388
  112.1 6.1 %collective-permute-start.1 = (f32[2560,128]{1,0:T(8,128)S(1)}, f32[2560,128]{1,0:T(8,128)S(1)}, u32[]{:S(2)}, u32[]{:S(2)}) collective-permute-start(f32[2560,128]{1,0:T(8,128)S(1)} %bitcast.10), channel_id=1, source_target_pairs={{0,1},{1,0},{2,3},{3,2},{4,5},{5,4},{6,7},{7,6},{8,9},{9,8},{10,11... | collective-permute-start | bytes 3932168 | tf_op jit(solution)/shard_map/ppermute | solution.py:370

commit v5 on v4

--- a/solution.py
+++ b/solution.py
@@ -19,7 +19,7 @@
 SB = 64
 HALF_TILES = 20
 SHARE = HALF_TILES * B // CHIPS
-CHUNK = SHARE + GROUP
+CHUNK = SHARE + 2 * GROUP
 f32 = jnp.float32
 bf16 = jnp.bfloat16
 ANY = pl.BlockSpec(memory_space=pl.ANY)
@@ -126,7 +126,7 @@
             pltpu.SemaphoreType.DMA((parts + 1,)),
             pltpu.SemaphoreType.DMA((2,)),
         ],
-        compiler_params=pltpu.CompilerParams(vmem_limit_bytes=16 << 20),
+        compiler_params=pltpu.CompilerParams(vmem_limit_bytes=60 << 20),
         name="transform",
     )(
         features,
@@ -135,11 +135,10 @@
     )
 
 
-def combine_kernel(p_ref, mine_ref, other_ref, x_ref):
-    core = lax.axis_index("rows") % 2
+def select_kernel(p_ref, rows_ref):
     mask = p_ref[:, COLS:].astype(f32)
-    row = lax.broadcasted_iota(jnp.int32, (ROWS_DEV, B), 0)
-    lane = lax.broadcasted_iota(jnp.int32, (ROWS_DEV, B), 1)
+    row = iota((ROWS_DEV, B), 0)
+    lane = iota((ROWS_DEV, B), 1)
     mask = jnp.where((row & (GROUP - 1)) == (lane & (GROUP - 1)), mask, 0.0).astype(bf16)
     shape = (DEVICES, DEVICES * GROUP)
     place = iota(shape, 0)
@@ -148,50 +147,69 @@
     block = jnp.where(target == source, 1.0, 0.0).astype(bf16)
     pick = dg(block, mask, 1, 0)
     mixer = (hadamard(target, source) * jnp.concatenate([pick] * GROUP, axis=1)).astype(bf16)
-    rows = dg(mixer, p_ref[:, :COLS], 1, 0) * (1.0 / math.sqrt(SAMPLES))
-    for b in range(NB):
-        for half in range(2):
-            x_ref[pl.ds(half * CHIPS * CHUNK + SHARE + b, CHIPS, stride=CHUNK), :] = rows[
-                half * CHIPS : (half + 1) * CHIPS, b * B : (b + 1) * B
-            ]
-    high, low = split(rows)
-    for r in range(NB):
-        left_high, left_low = high[:, r * B : (r + 1) * B], low[:, r * B : (r + 1) * B]
-        right_high, right_low = high[:, r * B :], low[:, r * B :]
-        gram = dg(left_high, right_high, 0, 0) + dg(left_high, right_low, 0, 0) + dg(left_low, right_high, 0, 0)
-        for c in range(r, NB):
-            half, spot = divmod(tile_index(r, c), HALF_TILES)
-            tile = gram[:, (c - r) * B : (c - r + 1) * B]
-            put_rows(x_ref, half, spot * B, tile)
-    for t in range(NB * (NB + 1) // 2, 2 * HALF_TILES):
-        half, spot = divmod(t, HALF_TILES)
-        put_rows(x_ref, half, spot * B, jnp.zeros((B, B), f32))
-    size = CHIPS * CHUNK
-    mine_ref[...] = x_ref[pl.ds(pl.multiple_of(core * size, 8), size), :]
-    other_ref[...] = x_ref[pl.ds(pl.multiple_of((1 - core) * size, 8), size), :]
-
-
-def put_rows(x_ref, half, start, tile):
+    rows_ref[...] = dg(mixer, p_ref[:, :COLS], 1, 0) * (1.0 / math.sqrt(SAMPLES))
+
+
+def select(pieces):
+    return pl.pallas_call(
+        select_kernel,
+        out_shape=jax.ShapeDtypeStruct((DEVICES, COLS), f32),
+        in_specs=[VMEM],
+        out_specs=VMEM,
+        compiler_params=pltpu.CompilerParams(vmem_limit_bytes=24 << 20),
+        name="select",
+    )(pieces)
+
+
+def put_rows(x_ref, start, tile):
     done = 0
     while done < B:
         chip, spot = divmod(start + done, SHARE)
         count = min(SHARE - spot, B - done)
-        base = (half * CHIPS + chip) * CHUNK + spot
+        base = chip * CHUNK + spot
         x_ref[base : base + count, :] = tile[done : done + count, :]
         done += count
 
 
-def combine(pieces):
-    shape = jax.ShapeDtypeStruct((CHIPS * CHUNK, B), f32)
+def gram_kernel(mine_ref, came_ref, x_ref, high_ref, low_ref):
+    core = lax.axis_index("rows") % 2
+    for j, ref in enumerate((mine_ref, came_ref)):
+        owned = ref[pl.ds(pl.multiple_of(core * CHIPS, CHIPS), CHIPS), :]
+        for b in range(NB):
+            x_ref[pl.ds(SHARE + GROUP * j + b, CHIPS, stride=CHUNK), :] = owned[:, b * B : (b + 1) * B]
+        high, low = split(ref[...])
+        high_ref[j * DEVICES : (j + 1) * DEVICES, :] = high
+        low_ref[j * DEVICES : (j + 1) * DEVICES, :] = low
+    count = NB * (NB + 1) // 2
+    for half in range(2):
+
+        @pl.when(core == half)
+        def _():
+            for r in range(NB):
+                inside = [
+                    c for c in range(r, NB) if half * HALF_TILES <= tile_index(r, c) < (half + 1) * HALF_TILES
+                ]
+                if not inside:
+                    continue
+                left = slice(r * B, (r + 1) * B)
+                right = slice(inside[0] * B, (inside[-1] + 1) * B)
+                gram = dot3((high_ref[:, left], low_ref[:, left]), (high_ref[:, right], low_ref[:, right]), 0, 0)
+                for n, c in enumerate(inside):
+                    put_rows(x_ref, (tile_index(r, c) - half * HALF_TILES) * B, gram[:, n * B : (n + 1) * B])
+            for t in range(count - half * HALF_TILES, HALF_TILES):
+                put_rows(x_ref, t * B, jnp.zeros((B, B), f32))
+
+
+def gram_share(mine, came):
     return pl.pallas_call(
-        combine_kernel,
-        out_shape=(shape, shape),
-        in_specs=[VMEM],
-        out_specs=(VMEM, VMEM),
-        scratch_shapes=[pltpu.VMEM((2 * CHIPS * CHUNK, B), f32)],
+        gram_kernel,
+        out_shape=jax.ShapeDtypeStruct((CHIPS * CHUNK, B), f32),
+        in_specs=[VMEM, VMEM],
+        out_specs=VMEM,
+        scratch_shapes=[pltpu.VMEM((2 * DEVICES, COLS), bf16)] * 2,
         compiler_params=pltpu.CompilerParams(vmem_limit_bytes=24 << 20),
-        name="combine",
-    )(pieces)
+        name="gram",
+    )(mine, came)
 
 
 def factor_rows(s_ref, i):
@@ -353,11 +371,9 @@
     pieces = lax.all_to_all(
         mixed.reshape(DEVICES, GROUP, COLS + B), "rows", split_axis=0, concat_axis=0, tiled=True
     ).reshape(ROWS_DEV, COLS + B)
-    mine, other = combine(pieces)
     swap = [(d, d ^ 1) for d in range(DEVICES)]
-    came = lax.ppermute(other, "rows", swap).reshape(CHIPS, CHUNK, B)
-    mine = mine.reshape(CHIPS, CHUNK, B)
-    shares = jnp.concatenate([mine[:, :SHARE] + came[:, :SHARE], mine[:, SHARE:], came[:, SHARE:]], axis=1)
+    rows = select(pieces)
+    shares = gram_share(rows, lax.ppermute(rows, "rows", swap)).reshape(CHIPS, CHUNK, B)
     same_core = [list(range(c, DEVICES, 2)) for c in range(2)]
     got = lax.all_to_all(
         shares, "rows", split_axis=0, concat_axis=0, tiled=True, axis_index_groups=same_core

time: 156 us -> 152 us (0.974)
  local copies, waits for them, and re-layouts: 3.07 us -> 0.1 us
    unnamed x10 -> x4, local copies, waits for them, and re-layouts: 2.94 us -> 0.01 us
where the time goes in v5:
time: 152 us; the launch traced here: 151 us
  blocking collectives  99.1 us (65%)
  Pallas kernels  42.3 us (28%)
  starting transfers between devices  4.79 us (3%)
  waiting for transfers between devices  4.2 us (3%)
    all_to_all x1, blocking collectives, shards(): lax.all_to_all(mixed.reshape(DEVICES, GROUP, COLS + B), 'rows', split_axi...  44.4 us
    pallas_call x1, Pallas kernels, factor(): pl.pallas_call(factor_kernel, out_shape=(jax.ShapeDtypeStruct((COLS, COLS...  37 us
    all_to_all x1, blocking collectives, shards(): lax.all_to_all(shares, 'rows', split_axis=0, concat_axis=0, tiled=True, a...  29.5 us
    all_to_all x1, blocking collectives, shards(): lax.all_to_all(jnp.broadcast_to(total[None], (CHIPS, SHARE, B)), 'rows',...  25.2 us
    pallas_call x1, Pallas kernels, transform(): pl.pallas_call(transform_kernel, out_shape=jax.ShapeDtypeStruct((ROWS_DEV...  3.71 us
    ppermute x1, starting transfers between devices, shards(): far = lax.ppermute(half, 'rows', swap)  3.42 us
  transfers between devices with their start and end apart: 2, of which 2 were waited for; matrix products, arithmetic and copies ran while one was open for 0% of the time, Pallas kernels for 0%

profile of v5, /device:TPU:1, one launch (start us, length us, event | category | flops | bytes accessed | tf_op | source)
XLA Modules:
  0.0 151.5 jit_solution(17598867416549199171)
XLA Ops:
  0.6 3.7 %transform.1 = bf16[1024,1152]{1,0:T(8,128)(2,1)} custom-call(bf16[1024,1024]{1,0:T(8,128)(2,1)} %f_hbm.1, s32[8,128]{1,0:T(8,128)} %bitcast.13, s32[1,32]{1,0:T(1,128)} %bitcast.11), custom_call_target="tpu_custom_call" | custom-call | tf_op jit(solution)/shard_map/transform/pallas_call | solution.py:115
  4.3 44.4 %all_to_all.15 = bf16[128,8,1152]{2,1,0:T(8,128)(2,1)S(1)} all-to-all(bf16[128,8,1152]{2,1,0:T(8,128)(2,1)} %bitcast.12), channel_id=1, replica_groups=mesh['rows'=128] {'rows'}, dimensions={0} | all-to-all | bytes 4718592 | tf_op jit(solution)/shard_map/all_to_all | solution.py:371
  48.8 0.7 select.1.mine_ref
  49.4 1.4 collective-permute-start
  50.8 1.5 %collective-permute-done.came_ref = f32[128,1024]{1,0:T(8,128)S(1)} collective-permute-done((f32[128,1024]{1,0:T(8,128)S(1)}, f32[128,1024]{1,0:T(8,128)S(1)}, u32[]{:S(2)}, u32[]{:S(2)}) %collective-permute-start) | collective-permute-done | bytes 524320 | tf_op jit(solution)/shard_map/ppermute | solution.py:376
  52.3 1.0 gram.1
  53.3 29.5 %all_to_all.16.got_ref = f32[64,56,128]{2,1,0:T(8,128)S(1)} all-to-all(f32[64,56,128]{2,1,0:T(8,128)S(1)} %bitcast.8), channel_id=1, replica_groups={{0,2,4,6,8,10,12,14,16,18,20,22,24,26,28,30,32,34,36,38,40,42,44,46,48,..., dimensions={0} | all-to-all | bytes 3670016 | tf_op jit(solution)/shard_map/all_to_all | solution.py:378
  82.8 0.1 slice_reduce_fusion
  82.9 0.0 copy-start
  83.0 0.0 copy-start.1
  83.0 0.1 broadcast_in_dim.2
  83.1 25.2 %all_to_all.17 = f32[64,40,128]{2,1,0:T(8,128)S(1)} all-to-all(f32[64,40,128]{2,1,0:T(8,128)S(1)} %broadcast_in_dim.2), channel_id=1, replica_groups={{0,2,4,6,8,10,12,14,16,18,20,22,24,26,28,30,32,34,36,38,40,42,44,46,48,..., dimensions={0} | all-to-all | bytes 2621440 | tf_op jit(solution)/shard_map/all_to_all | solution.py:382
  108.2 3.4 %collective-permute-start.1 = (f32[2560,128]{1,0:T(8,128)S(1)}, f32[2560,128]{1,0:T(8,128)S(1)}, u32[]{:S(2)}, u32[]{:S(2)}) collective-permute-start(f32[2560,128]{1,0:T(8,128)S(1)} %bitcast.9), channel_id=1, source_target_pairs={{0,1},{1,0},{2,3},{3,2},{4,5},{5,4},{6,7},{7,6},{8,9},{9,8},{10,11... | collective-permute-start | bytes 3932168 | tf_op jit(solution)/shard_map/ppermute | solution.py:386
  111.6 2.7 %collective-permute-done.1.other_ref = f32[2560,128]{1,0:T(8,128)S(1)} collective-permute-done((f32[2560,128]{1,0:T(8,128)S(1)}, f32[2560,128]{1,0:T(8,128)S(1)}, u32[]{:S(2)}, u32[]{:S(2)}) %collective-permute-start.1) | collective-permute-done | bytes 1310752 | tf_op jit(solution)/shard_map/ppermute | solution.py:386
  114.3 0.0 copy-done
  114.3 0.0 copy-done.1
  114.3 37.0 %factor.1 = (f32[1024,1024]{1,0:T(8,128)}, f32[1,1024]{1,0:T(1,128)}, f32[32,1024]{1,0:T(8,128)}) custom-call(s32[32]{0:T(128)S(1)} %copy-done.1, f32[2560,128]{1,0:T(8,128)S(1)} %bitcast.10, f32[2560,128]{1,0:T(8,128)S(1)} %collective-permute-done.1.other_ref, f32[64,56,128]{2,1,0:T(8,128)S(1)} %all_to_all.16.got_ref, bf16[1024,1024]{1,0:T(8,128)(2,1)S(1)} %copy-done), custom_call_target="tpu_custom_call" | custom-call | tf_op jit(solution)/shard_map/factor/pallas_call | solution.py:344
Async XLA Ops:
  49.4 2.9 %collective-permute-start = (f32[128,1024]{1,0:T(8,128)S(1)}, f32[128,1024]{1,0:T(8,128)S(1)}, u32[]{:S(2)}, u32[]{:S(2)}) collective-permute-start(f32[128,1024]{1,0:T(8,128)S(1)} %select.1.mine_ref), channel_id=1, source_target_pairs={{0,1},{1,0},{2,3},{3,2},{4,5},{5,4},{6,7},{7,6},{8,9},{9,8},{10,11... | collective-permute-start | bytes 1572872 | tf_op jit(solution)/shard_map/ppermute | solution.py:376
  82.9 31.4 %copy-start = (bf16[1024,1024]{1,0:T(8,128)(2,1)S(1)}, bf16[1024,1024]{1,0:T(8,128)(2,1)}, u32[]{:S(2)}) copy-start(bf16[1024,1024]{1,0:T(8,128)(2,1)} %f_hbm.1) | copy-start | bytes 6291460
  83.0 31.4 %copy-start.1 = (s32[32]{0:T(128)S(1)}, s32[32]{0:T(128)}, u32[]{:S(2)}) copy-start(s32[32]{0:T(128)} %sample_ref.1) | copy-start | bytes 388
  108.2 6.1 %collective-permute-start.1 = (f32[2560,128]{1,0:T(8,128)S(1)}, f32[2560,128]{1,0:T(8,128)S(1)}, u32[]{:S(2)}, u32[]{:S(2)}) collective-permute-start(f32[2560,128]{1,0:T(8,128)S(1)} %bitcast.9), channel_id=1, source_target_pairs={{0,1},{1,0},{2,3},{3,2},{4,5},{5,4},{6,7},{7,6},{8,9},{9,8},{10,11... | collective-permute-start | bytes 3932168 | tf_op jit(solution)/shard_map/ppermute | solution.py:386

commit v6 on v5

--- a/solution.py
+++ b/solution.py
@@ -280,7 +280,7 @@
     if p % 2:
         pair = slice(o - B, e)
         w = dg(f_ref[:, :e], xh_ref[:e, pair], 1, 0) + dg(f_ref[:, :e], xl_ref[:e, pair], 1, 0)
-        acc_ref[...] += w * w
+        acc_ref[...] = w * w if p == 1 else acc_ref[...] + w * w
 
 
 def factor_kernel(
@@ -305,8 +305,8 @@
             own = mine_ref[spot * B : (spot + 1) * B, :]
             far = other_ref[spot * B : (spot + 1) * B, :]
             a_ref[r * B : (r + 1) * B, c * B : (c + 1) * B] = jnp.where(first == (half == 0), own, far)
-    u_ref[...] = jnp.zeros_like(u_ref)
-    acc_ref[...] = jnp.zeros_like(acc_ref)
+    for r in range(1, NB):
+        u_ref[r * B : (r + 1) * B, : r * B] = jnp.zeros((B, r * B), f32)
     ri = lax.broadcasted_iota(jnp.int32, (B, B), 0)
     ci = lax.broadcasted_iota(jnp.int32, (B, B), 1)
 

time: 152 us -> 152 us (level)
  no operation moved by 1% of the time
where the time goes in v6:
time: 152 us; the launch traced here: 151 us
  blocking collectives  99.1 us (65%)
  Pallas kernels  42.2 us (28%)
  starting transfers between devices  4.79 us (3%)
  waiting for transfers between devices  4.2 us (3%)
    all_to_all x1, blocking collectives, shards(): lax.all_to_all(mixed.reshape(DEVICES, GROUP, COLS + B), 'rows', split_axi...  44.4 us
    pallas_call x1, Pallas kernels, factor(): pl.pallas_call(factor_kernel, out_shape=(jax.ShapeDtypeStruct((COLS, COLS...  36.9 us
    all_to_all x1, blocking collectives, shards(): lax.all_to_all(shares, 'rows', split_axis=0, concat_axis=0, tiled=True, a...  29.5 us
    all_to_all x1, blocking collectives, shards(): lax.all_to_all(jnp.broadcast_to(total[None], (CHIPS, SHARE, B)), 'rows',...  25.2 us
    pallas_call x1, Pallas kernels, transform(): pl.pallas_call(transform_kernel, out_shape=jax.ShapeDtypeStruct((ROWS_DEV...  3.71 us
    ppermute x1, starting transfers between devices, shards(): far = lax.ppermute(half, 'rows', swap)  3.42 us
  transfers between devices with their start and end apart: 2, of which 2 were waited for; matrix products, arithmetic and copies ran while one was open for 0% of the time, Pallas kernels for 0%

profile of v6, /device:TPU:1, one launch (start us, length us, event | category | flops | bytes accessed | tf_op | source)
XLA Modules:
  0.0 151.4 jit_solution(644686940500497807)
XLA Ops:
  0.6 3.7 %transform.1 = bf16[1024,1152]{1,0:T(8,128)(2,1)} custom-call(bf16[1024,1024]{1,0:T(8,128)(2,1)} %f_hbm.1, s32[8,128]{1,0:T(8,128)} %bitcast.13, s32[1,32]{1,0:T(1,128)} %bitcast.11), custom_call_target="tpu_custom_call" | custom-call | tf_op jit(solution)/shard_map/transform/pallas_call | solution.py:115
  4.3 44.4 %all_to_all.15 = bf16[128,8,1152]{2,1,0:T(8,128)(2,1)S(1)} all-to-all(bf16[128,8,1152]{2,1,0:T(8,128)(2,1)} %bitcast.12), channel_id=1, replica_groups=mesh['rows'=128] {'rows'}, dimensions={0} | all-to-all | bytes 4718592 | tf_op jit(solution)/shard_map/all_to_all | solution.py:371
  48.8 0.7 select.1.mine_ref
  49.4 1.4 collective-permute-start
  50.8 1.5 %collective-permute-done.came_ref = f32[128,1024]{1,0:T(8,128)S(1)} collective-permute-done((f32[128,1024]{1,0:T(8,128)S(1)}, f32[128,1024]{1,0:T(8,128)S(1)}, u32[]{:S(2)}, u32[]{:S(2)}) %collective-permute-start) | collective-permute-done | bytes 524320 | tf_op jit(solution)/shard_map/ppermute | solution.py:376
  52.3 1.0 gram.1
  53.3 29.5 %all_to_all.16.got_ref = f32[64,56,128]{2,1,0:T(8,128)S(1)} all-to-all(f32[64,56,128]{2,1,0:T(8,128)S(1)} %bitcast.8), channel_id=1, replica_groups={{0,2,4,6,8,10,12,14,16,18,20,22,24,26,28,30,32,34,36,38,40,42,44,46,48,..., dimensions={0} | all-to-all | bytes 3670016 | tf_op jit(solution)/shard_map/all_to_all | solution.py:378
  82.8 0.1 slice_reduce_fusion
  82.9 0.0 copy-start
  83.0 0.0 copy-start.1
  83.0 0.1 broadcast_in_dim.2
  83.1 25.2 %all_to_all.17 = f32[64,40,128]{2,1,0:T(8,128)S(1)} all-to-all(f32[64,40,128]{2,1,0:T(8,128)S(1)} %broadcast_in_dim.2), channel_id=1, replica_groups={{0,2,4,6,8,10,12,14,16,18,20,22,24,26,28,30,32,34,36,38,40,42,44,46,48,..., dimensions={0} | all-to-all | bytes 2621440 | tf_op jit(solution)/shard_map/all_to_all | solution.py:382
  108.2 3.4 %collective-permute-start.1 = (f32[2560,128]{1,0:T(8,128)S(1)}, f32[2560,128]{1,0:T(8,128)S(1)}, u32[]{:S(2)}, u32[]{:S(2)}) collective-permute-start(f32[2560,128]{1,0:T(8,128)S(1)} %bitcast.9), channel_id=1, source_target_pairs={{0,1},{1,0},{2,3},{3,2},{4,5},{5,4},{6,7},{7,6},{8,9},{9,8},{10,11... | collective-permute-start | bytes 3932168 | tf_op jit(solution)/shard_map/ppermute | solution.py:386
  111.6 2.7 %collective-permute-done.1.other_ref = f32[2560,128]{1,0:T(8,128)S(1)} collective-permute-done((f32[2560,128]{1,0:T(8,128)S(1)}, f32[2560,128]{1,0:T(8,128)S(1)}, u32[]{:S(2)}, u32[]{:S(2)}) %collective-permute-start.1) | collective-permute-done | bytes 1310752 | tf_op jit(solution)/shard_map/ppermute | solution.py:386
  114.3 0.0 copy-done
  114.3 0.0 copy-done.1
  114.3 36.9 %factor.1 = (f32[1024,1024]{1,0:T(8,128)}, f32[1,1024]{1,0:T(1,128)}, f32[32,1024]{1,0:T(8,128)}) custom-call(s32[32]{0:T(128)S(1)} %copy-done.1, f32[2560,128]{1,0:T(8,128)S(1)} %bitcast.10, f32[2560,128]{1,0:T(8,128)S(1)} %collective-permute-done.1.other_ref, f32[64,56,128]{2,1,0:T(8,128)S(1)} %all_to_all.16.got_ref, bf16[1024,1024]{1,0:T(8,128)(2,1)S(1)} %copy-done), custom_call_target="tpu_custom_call" | custom-call | tf_op jit(solution)/shard_map/factor/pallas_call | solution.py:344
Async XLA Ops:
  49.4 2.9 %collective-permute-start = (f32[128,1024]{1,0:T(8,128)S(1)}, f32[128,1024]{1,0:T(8,128)S(1)}, u32[]{:S(2)}, u32[]{:S(2)}) collective-permute-start(f32[128,1024]{1,0:T(8,128)S(1)} %select.1.mine_ref), channel_id=1, source_target_pairs={{0,1},{1,0},{2,3},{3,2},{4,5},{5,4},{6,7},{7,6},{8,9},{9,8},{10,11... | collective-permute-start | bytes 1572872 | tf_op jit(solution)/shard_map/ppermute | solution.py:376
  82.9 31.4 %copy-start = (bf16[1024,1024]{1,0:T(8,128)(2,1)S(1)}, bf16[1024,1024]{1,0:T(8,128)(2,1)}, u32[]{:S(2)}) copy-start(bf16[1024,1024]{1,0:T(8,128)(2,1)} %f_hbm.1) | copy-start | bytes 6291460
  83.0 31.4 %copy-start.1 = (s32[32]{0:T(128)S(1)}, s32[32]{0:T(128)}, u32[]{:S(2)}) copy-start(s32[32]{0:T(128)} %sample_ref.1) | copy-start | bytes 388
  108.2 6.1 %collective-permute-start.1 = (f32[2560,128]{1,0:T(8,128)S(1)}, f32[2560,128]{1,0:T(8,128)S(1)}, u32[]{:S(2)}, u32[]{:S(2)}) collective-permute-start(f32[2560,128]{1,0:T(8,128)S(1)} %bitcast.9), channel_id=1, source_target_pairs={{0,1},{1,0},{2,3},{3,2},{4,5},{5,4},{6,7},{7,6},{8,9},{9,8},{10,11... | collective-permute-start | bytes 3932168 | tf_op jit(solution)/shard_map/ppermute | solution.py:386
